TPU v7x, 32 devices: a whole 2x2x4 slice. The times are simulated.
32 devices in a mesh: dp: 8 (over y, x, core), tensor: 4 (over z).
Axes of the slice: x: 2, y: 2, z: 4, core: 2. Of those that a mesh axis runs over, the one named last changes fastest.
Arguments:
- tokens: bfloat16 [8192, 768], P(('dp', 'tensor')), may hold values from -60 to 60
- encoder: bfloat16 [4096, 768], P(('dp', 'tensor')), may hold values from -6 to 6
- segments: int32 [8, 1024], P('dp'), may hold values from 0 to 5, never falling along the last dimension, each value on 1 to 800 neighbouring positions
- rel_bucket: int32 [1024], replicated, may hold values from 0 to 31
- out_grad: bfloat16 [8192, 768], P(('dp', 'tensor')), may hold values from -6 to 6
- self_q: bfloat16 [768, 768], P('dp', 'tensor'), may hold values from -0.109375 to 0.109375
- self_k: bfloat16 [768, 768], P('dp', 'tensor'), may hold values from -0.109375 to 0.109375
- self_v: bfloat16 [768, 768], P('dp', 'tensor'), may hold values from -0.21875 to 0.21875
- self_o: bfloat16 [768, 768], P('tensor', 'dp'), may hold values from -0.875 to 0.875
- cross_q: bfloat16 [768, 768], P('dp', 'tensor'), may hold values from -0.109375 to 0.109375
- cross_k: bfloat16 [768, 768], P('dp', 'tensor'), may hold values from -0.109375 to 0.109375
- cross_v: bfloat16 [768, 768], P('dp', 'tensor'), may hold values from -0.21875 to 0.21875
- cross_o: bfloat16 [768, 768], P('tensor', 'dp'), may hold values from -0.875 to 0.875
- ffn_gate: bfloat16 [768, 2048], P('dp', 'tensor'), may hold values from -0.21875 to 0.21875
- ffn_up: bfloat16 [768, 2048], P('dp', 'tensor'), may hold values from -0.21875 to 0.21875
- ffn_down: bfloat16 [2048, 768], P('tensor', 'dp'), may hold values from -0.125 to 0.125
- bias_table: bfloat16 [32, 12], P(None, 'tensor'), may hold values from -3 to 3
- norm_gains: bfloat16 [3, 768], P(None, 'dp'), may hold values from 0.5 to 1.5
Outputs:
- layer_out: bfloat16 [8192, 768], P(('dp', 'tensor'))
- tokens_grad: float32 [8192, 768], P(('dp', 'tensor'))
- encoder_grad: float32 [4096, 768], P(('dp', 'tensor'))
- self_q_grad: float32 [768, 768], P('dp', 'tensor')
- self_k_grad: float32 [768, 768], P('dp', 'tensor')
- self_v_grad: float32 [768, 768], P('dp', 'tensor')
- self_o_grad: float32 [768, 768], P('tensor', 'dp')
- cross_q_grad: float32 [768, 768], P('dp', 'tensor')
- cross_k_grad: float32 [768, 768], P('dp', 'tensor')
- cross_v_grad: float32 [768, 768], P('dp', 'tensor')
- cross_o_grad: float32 [768, 768], P('tensor', 'dp')
- ffn_gate_grad: float32 [768, 2048], P('dp', 'tensor')
- ffn_up_grad: float32 [768, 2048], P('dp', 'tensor')
- ffn_down_grad: float32 [2048, 768], P('tensor', 'dp')
- bias_table_grad: float32 [32, 12], P(None, 'tensor')
- norm_gains_grad: float32 [3, 768], P(None, 'dp')
Inputs may be any that keep to these rules, and one draw needn't show every extreme that they name: `segments`: within each sequence the numbers never fall; every document holds at most 800 tokens and some holds exactly 800.
All inputs are finite; a program needn't handle non-finite values.
Results may differ from a plain program's by a relative error of at most 0.04.
Values may be sent and summed in bfloat16 or wider, within the bound.
A program may use at most 192 MiB of HBM per device.

v0:
```python
from functools import partial

import jax
import jax.numpy as jnp
from jax import lax
from jax.sharding import PartitionSpec as P

HEADS = 12
DK = 64
NB = 32
LEN = 1024
ENC = 512


EPS = 1e-06
MASKED = -1e30
HIGHEST = lax.Precision.HIGHEST


def product(left, right):
    return jnp.dot(left, right, preferred_element_type=jnp.float32)


def product_tn(left, right):
    return lax.dot_general(
        left, right, (((0,), (0,)), ((), ())), preferred_element_type=jnp.float32
    )


def product_nt(left, right):
    return lax.dot_general(
        left, right, (((1,), (1,)), ((), ())), preferred_element_type=jnp.float32
    )


def norm_forward(rows, gain):
    scale = lax.rsqrt(jnp.mean(rows * rows, axis=-1, keepdims=True) + EPS)
    return (rows * scale * gain, scale)


def norm_backward(rows, scale, gain, upstream):
    weighted = upstream * gain
    inner = jnp.mean(weighted * rows, axis=-1, keepdims=True)
    grad_rows = scale * weighted - rows * scale * scale * scale * inner
    grad_gain = jnp.sum(upstream * rows * scale, axis=0)
    return (grad_rows, grad_gain)


def gather_rows(value):
    return lax.all_gather(value, "tensor", axis=0, tiled=True)


def scatter_rows(term, count):
    return lax.psum_scatter(
        term(jnp.int32(0), lax.axis_size("tensor") * count).astype(jnp.bfloat16),
        "tensor",
        scatter_dimension=0,
        tiled=True,
    ).astype(jnp.float32)


def gated(gate, upper):
    return jax.nn.gelu(gate, approximate=True) * upper


def split_heads(value):
    return value.reshape(value.shape[0], value.shape[1] // DK, DK)


def skewed_grid(line, block, length):
    heads = line.shape[0]
    width = line.shape[1]
    tiled = jnp.tile(line, (1, block + 1))[:, : block * (width + 1)]
    grid = tiled.reshape(heads, block, width + 1)[:, :, :length]
    return grid[:, :, ::-1]


def diagonal_sums(grid, width):
    heads, block, length = grid.shape
    flipped = grid[:, :, ::-1]
    padded = jnp.pad(flipped, ((0, 0), (0, 0), (0, width + 1 - length)))
    flat = padded.reshape(heads, block * (width + 1))
    flat = jnp.pad(flat, ((0, 0), (0, (block + 1) * width - block * (width + 1))))
    return jnp.sum(flat.reshape(heads, block + 1, width), axis=1)


def self_scores(query, start, keys, segment_ids, bias_line):
    block = query.shape[0]
    length = keys.shape[0]
    rows = start + jnp.arange(block, dtype=jnp.int32)
    columns = jnp.arange(length, dtype=jnp.int32)
    distance = rows[:, None] - columns[None, :]
    valid = (distance >= 0) & (segment_ids[start : start + block][:, None] == segment_ids[None, :])
    width = block + length
    scores = jnp.einsum("qhd,khd->hqk", query, keys, preferred_element_type=jnp.float32)
    scores = scores + skewed_grid(bias_line[:, start : start + width], block, length)
    return (jnp.where(valid[None], scores, MASKED), True)


def cross_scores(query, start, keys):
    return (jnp.einsum("qhd,khd->hqk", query, keys, preferred_element_type=jnp.float32), False)


def attend(query, values, score_fn):
    length = query.shape[0]
    block = min(512, length)
    outputs = []
    totals = []
    for start in range(0, length, block):
        scores, unused = score_fn(query[start : start + block], start)
        highest = jnp.max(scores, axis=-1, keepdims=True)
        total = highest + jnp.log(jnp.sum(jnp.exp(scores - highest), axis=-1, keepdims=True))
        weights = jnp.exp(scores - total).astype(jnp.bfloat16)
        outputs.append(
            jnp.einsum("hqk,khd->qhd", weights, values, preferred_element_type=jnp.float32)
        )
        totals.append(total)
    return (jnp.concatenate(outputs, 0), totals)


def attend_back(query, keys, values, upstream, totals, score_fn, distance_grad):
    length = query.shape[0]
    key_count = keys.shape[0]
    block = min(512, length)
    width = block + key_count
    grad_keys = jnp.zeros(keys.shape, jnp.float32)
    grad_values = jnp.zeros(values.shape, jnp.float32)
    grad_queries = []
    for number, start in enumerate(range(0, length, block)):
        part = query[start : start + block]
        scores, with_bias = score_fn(part, start)
        probs = jnp.exp(scores - totals[number])
        above = upstream[start : start + block]
        grad_probs = jnp.einsum("qhd,khd->hqk", above, values, preferred_element_type=jnp.float32)
        inner = jnp.sum(probs * grad_probs, axis=-1, keepdims=True)
        grad_scores = (probs * (grad_probs - inner)).astype(jnp.bfloat16)
        grad_queries.append(
            jnp.einsum("hqk,khd->qhd", grad_scores, keys, preferred_element_type=jnp.float32)
        )
        grad_keys = grad_keys + jnp.einsum(
            "hqk,qhd->khd", grad_scores, part, preferred_element_type=jnp.float32
        )
        grad_values = grad_values + jnp.einsum(
            "hqk,qhd->khd", probs.astype(jnp.bfloat16), above, preferred_element_type=jnp.float32
        )
        if with_bias:
            sums = diagonal_sums(grad_scores.astype(jnp.float32), width)
            distance_grad = distance_grad.at[:, start : start + width].add(sums)
    return (jnp.concatenate(grad_queries, 0), grad_keys, grad_values, distance_grad)


def per_device(
    tokens,
    encoder,
    segments,
    rel_bucket,
    out_grad,
    self_q,
    self_k,
    self_v,
    self_o,
    cross_q,
    cross_k,
    cross_v,
    cross_o,
    ffn_gate,
    ffn_up,
    ffn_down,
    bias_table,
    norm_gains,
):
    half = jnp.bfloat16
    gathered = tuple(
        (
            lax.all_gather(self_q, "dp", axis=0, tiled=True),
            lax.all_gather(self_k, "dp", axis=0, tiled=True),
            lax.all_gather(self_v, "dp", axis=0, tiled=True),
            lax.all_gather(self_o, "dp", axis=1, tiled=True),
            lax.all_gather(cross_q, "dp", axis=0, tiled=True),
            lax.all_gather(cross_k, "dp", axis=0, tiled=True),
            lax.all_gather(cross_v, "dp", axis=0, tiled=True),
            lax.all_gather(cross_o, "dp", axis=1, tiled=True),
            lax.all_gather(ffn_gate, "dp", axis=0, tiled=True),
            lax.all_gather(ffn_up, "dp", axis=0, tiled=True),
            lax.all_gather(ffn_down, "dp", axis=1, tiled=True),
            lax.all_gather(norm_gains, "dp", axis=1, tiled=True),
        )
    )
    (
        query_w,
        key_w,
        value_w,
        output_w,
        cross_query_w,
        cross_key_w,
        cross_value_w,
        cross_output_w,
        gate_shard,
        up_shard,
        down_shard,
        gains_half,
    ) = gathered
    gains = gains_half.astype(jnp.float32)
    heads = self_q.shape[1] // DK
    local_rows = tokens.shape[0]
    buckets = bias_table.shape[0]
    table_t = bias_table.astype(jnp.float32).T
    bucket_table = (rel_bucket[None, :] == jnp.arange(buckets, dtype=jnp.int32)[:, None]).astype(
        jnp.float32
    )
    distance_bias = jnp.dot(
        table_t, bucket_table, precision=HIGHEST, preferred_element_type=jnp.float32
    )
    block_rows = min(512, LEN)
    bias_line = jnp.pad(distance_bias, ((0, 0), (LEN - 1, block_rows)))
    residual = tokens.astype(jnp.float32)
    normed_self, scale_self = norm_forward(residual, gains[0])
    normed_self_all = gather_rows(normed_self.astype(half))
    query_self = product(normed_self_all, query_w).astype(half)
    key_self = product(normed_self_all, key_w).astype(half)
    value_self = product(normed_self_all, value_w).astype(half)
    number = 0
    score_fn = partial(
        self_scores, keys=split_heads(key_self), segment_ids=segments[number], bias_line=bias_line
    )
    output, totals = attend(split_heads(query_self), split_heads(value_self), score_fn)
    attn_parts = output.reshape(LEN, heads * DK)
    self_totals = [totals]
    self_score_fns = [score_fn]
    attn_self = attn_parts.astype(half)

    def self_out_rows(start, count):
        return product(attn_self, output_w)

    hidden_one = residual + scatter_rows(self_out_rows, local_rows)
    normed_cross, scale_cross = norm_forward(hidden_one, gains[1])
    normed_cross_all = gather_rows(normed_cross.astype(half))
    encoder_all = lax.all_gather(encoder, "tensor", axis=0, tiled=True)
    query_cross = product(normed_cross_all, cross_query_w).astype(half)
    key_cross = product(encoder_all, cross_key_w).astype(half)
    value_cross = product(encoder_all, cross_value_w).astype(half)
    score_fn = partial(cross_scores, keys=split_heads(key_cross))
    output, totals = attend(split_heads(query_cross), split_heads(value_cross), score_fn)
    cross_parts = output.reshape(LEN, heads * DK)
    cross_totals = [totals]
    cross_score_fns = [score_fn]
    attn_cross = cross_parts.astype(half)

    def cross_out_rows(start, count):
        return product(attn_cross, cross_output_w)

    hidden_two = hidden_one + scatter_rows(cross_out_rows, local_rows)
    normed_ffn, scale_ffn = norm_forward(hidden_two, gains[2])
    normed_ffn_half = normed_ffn.astype(half)
    ffn_rows = gather_rows(normed_ffn_half)
    gate_w, up_w, down_w = (gate_shard, up_shard, down_shard)
    gate = product(ffn_rows, gate_w)
    upper = product(ffn_rows, up_w)
    inner = gated(gate, upper).astype(half)

    def ffn_out_rows(start, count):
        return product(inner, down_w)

    ffn_out = scatter_rows(ffn_out_rows, local_rows)
    layer_out = (hidden_two + ffn_out).astype(half)
    upstream = out_grad.astype(jnp.float32)
    grad_rows = gather_rows(out_grad)
    grad_down = product_tn(inner, grad_rows)
    grad_inner = product_nt(grad_rows, down_w)
    unused, pull = jax.vjp(gated, gate, upper)
    grad_gate, grad_up = pull(grad_inner)
    grad_gate = grad_gate.astype(half)
    grad_up = grad_up.astype(half)
    grad_gate_w = product_tn(ffn_rows, grad_gate)
    grad_up_w = product_tn(ffn_rows, grad_up)

    def ffn_back_rows(start, count):
        return product_nt(grad_gate, gate_w) + product_nt(grad_up, up_w)

    grad_normed_ffn = scatter_rows(ffn_back_rows, local_rows)
    back_ffn, gain_grad_ffn = norm_backward(hidden_two, scale_ffn, gains[2], grad_normed_ffn)
    grad_two = upstream + back_ffn
    grad_two_all = gather_rows(grad_two.astype(half))
    grad_cross_output = product_tn(attn_cross, grad_two_all)
    grad_attn_cross = product_nt(grad_two_all, cross_output_w).astype(half)
    empty_line = jnp.zeros(bias_line.shape, jnp.float32)
    number = 0
    grad_query, grad_key, grad_value, unused_line = attend_back(
        split_heads(query_cross),
        split_heads(key_cross),
        split_heads(value_cross),
        split_heads(grad_attn_cross),
        cross_totals[number],
        cross_score_fns[number],
        empty_line,
    )
    cross_queries = grad_query.reshape(LEN, heads * DK)
    cross_keys = grad_key.reshape(ENC, heads * DK)
    cross_values = grad_value.reshape(ENC, heads * DK)
    grad_query_cross = cross_queries.astype(half)
    grad_key_cross = cross_keys.astype(half)
    grad_value_cross = cross_values.astype(half)
    grad_cross_query = product_tn(normed_cross_all, grad_query_cross)
    grad_cross_key = product_tn(encoder_all, grad_key_cross)
    grad_cross_value = product_tn(encoder_all, grad_value_cross)

    def cross_back_rows(start, count):
        return product_nt(grad_query_cross, cross_query_w)

    grad_normed_cross = scatter_rows(cross_back_rows, local_rows)
    encoder_grad = lax.psum_scatter(
        (
            product_nt(grad_key_cross, cross_key_w) + product_nt(grad_value_cross, cross_value_w)
        ).astype(jnp.bfloat16),
        "tensor",
        scatter_dimension=0,
        tiled=True,
    ).astype(jnp.float32)
    back_cross, gain_grad_cross = norm_backward(
        hidden_one, scale_cross, gains[1], grad_normed_cross
    )
    grad_one = grad_two + back_cross
    grad_one_all = gather_rows(grad_one.astype(half))
    grad_self_output = product_tn(attn_self, grad_one_all)
    grad_attn_self = product_nt(grad_one_all, output_w).astype(half)
    distance_grad = empty_line
    number = 0
    grad_query, grad_key, grad_value, distance_grad = attend_back(
        split_heads(query_self),
        split_heads(key_self),
        split_heads(value_self),
        split_heads(grad_attn_self),
        self_totals[number],
        self_score_fns[number],
        distance_grad,
    )
    self_queries = grad_query.reshape(LEN, heads * DK)
    self_keys = grad_key.reshape(LEN, heads * DK)
    self_values = grad_value.reshape(LEN, heads * DK)
    grad_query_self = self_queries.astype(half)
    grad_key_self = self_keys.astype(half)
    grad_value_self = self_values.astype(half)
    grad_self_query = product_tn(normed_self_all, grad_query_self)
    grad_self_key = product_tn(normed_self_all, grad_key_self)
    grad_self_value = product_tn(normed_self_all, grad_value_self)
    table_grad = product_nt(distance_grad[:, LEN - 1 : 2 * LEN - 1], bucket_table).T

    def self_back_rows(start, count):
        total = product_nt(grad_query_self, query_w)
        total = total + product_nt(grad_key_self, key_w)
        return total + product_nt(grad_value_self, value_w)

    grad_normed_self = scatter_rows(self_back_rows, local_rows)
    back_self, gain_grad_self = norm_backward(residual, scale_self, gains[0], grad_normed_self)
    tokens_grad = grad_one + back_self
    tensor_pos = lax.axis_index("tensor")
    table_full = lax.dynamic_update_slice(
        jnp.zeros((NB, HEADS), jnp.float32), table_grad, (0, tensor_pos * heads)
    )
    gain_grads = jnp.stack([gain_grad_self, gain_grad_cross, gain_grad_ffn])
    gain_sum, table_sum = lax.psum((gain_grads, table_full), ("dp", "tensor"))
    width = gain_sum.shape[1] // lax.axis_size("dp")
    norm_gains_grad = lax.dynamic_slice_in_dim(gain_sum, lax.axis_index("dp") * width, width, 1)
    bias_table_grad = lax.dynamic_slice_in_dim(table_sum, tensor_pos * heads, heads, 1)
    reduced = (
        lax.psum_scatter(grad_self_query, "dp", scatter_dimension=0, tiled=True),
        lax.psum_scatter(grad_self_key, "dp", scatter_dimension=0, tiled=True),
        lax.psum_scatter(grad_self_value, "dp", scatter_dimension=0, tiled=True),
        lax.psum_scatter(grad_self_output, "dp", scatter_dimension=1, tiled=True),
        lax.psum_scatter(grad_cross_query, "dp", scatter_dimension=0, tiled=True),
        lax.psum_scatter(grad_cross_key, "dp", scatter_dimension=0, tiled=True),
        lax.psum_scatter(grad_cross_value, "dp", scatter_dimension=0, tiled=True),
        lax.psum_scatter(grad_cross_output, "dp", scatter_dimension=1, tiled=True),
        lax.psum_scatter(grad_gate_w, "dp", scatter_dimension=0, tiled=True),
        lax.psum_scatter(grad_up_w, "dp", scatter_dimension=0, tiled=True),
        lax.psum_scatter(grad_down, "dp", scatter_dimension=1, tiled=True),
    )
    return (
        layer_out,
        tokens_grad,
        encoder_grad,
        reduced[0],
        reduced[1],
        reduced[2],
        reduced[3],
        reduced[4],
        reduced[5],
        reduced[6],
        reduced[7],
        reduced[8],
        reduced[9],
        reduced[10],
        bias_table_grad,
        norm_gains_grad,
    )


def solution(mesh):
    placed = (
        P(("dp", "tensor"), None),
        P(("dp", "tensor"), None),
        P("dp", None),
        P(),
        P(("dp", "tensor"), None),
        P("dp", "tensor"),
        P("dp", "tensor"),
        P("dp", "tensor"),
        P("tensor", "dp"),
        P("dp", "tensor"),
        P("dp", "tensor"),
        P("dp", "tensor"),
        P("tensor", "dp"),
        P("dp", "tensor"),
        P("dp", "tensor"),
        P("tensor", "dp"),
        P(None, "tensor"),
        P(None, "dp"),
    )
    return jax.shard_map(
        per_device,
        mesh=mesh,
        in_specs=placed,
        out_specs=(
            P(("dp", "tensor"), None),
            P(("dp", "tensor"), None),
            P(("dp", "tensor"), None),
            P("dp", "tensor"),
            P("dp", "tensor"),
            P("dp", "tensor"),
            P("tensor", "dp"),
            P("dp", "tensor"),
            P("dp", "tensor"),
            P("dp", "tensor"),
            P("tensor", "dp"),
            P("dp", "tensor"),
            P("dp", "tensor"),
            P("tensor", "dp"),
            P(None, "tensor"),
            P(None, "dp"),
        ),
        check_vma=False,
    )
```

profile of v0, /device:TPU:0, one launch (start us, length us, event | category | flops | bytes accessed | tf_op | source)
XLA Modules:
  0.0 1230.1 jit_solution(15191541748346808265)
XLA Ops:
  8.4 10.6 all-gather
  22.9 5.4 broadcast_bitcast_fusion
  28.3 21.7 %copy.98 = f32[1,3,513,1536]{3,1,2,0:T(4,128)S(1)} copy(f32[1,3,513,1536]{3,2,1,0:T(8,128)S(1)} %get-tuple-element.151) | data formatting | bytes 18911232
  50.0 4.9 slice.171
  54.9 13.2 %reshape.359 = f32[2360832]{0:T(1024)} reshape(f32[3,786944]{1,0:T(4,128)} %slice.171) | data formatting | bytes 18886656
  68.2 16.9 %reshape.338 = f32[3,512,1537]{2,1,0:T(8,128)} reshape(f32[2360832]{0:T(1024)} %reshape.359) | data formatting | bytes 18886656 | tf_op jit(solution)/shard_map/reshape | solution.py:74
  85.0 6.5 slice.172
  91.6 51.0 %rev.15 = f32[3,512,1024]{2,1,0:T(8,128)} reverse(f32[3,512,1024]{2,1,0:T(8,128)} %slice.172), dimensions={2} | reverse | bytes 12582912 | tf_op jit(solution)/shard_map/rev | solution.py:75
  142.6 11.3 copy.97
  153.8 4.9 slice.168
  158.8 13.2 %reshape.361 = f32[2360832]{0:T(1024)} reshape(f32[3,786944]{1,0:T(4,128)} %slice.168) | data formatting | bytes 18886656
  172.0 16.6 %reshape.337 = f32[3,512,1537]{2,1,0:T(8,128)} reshape(f32[2360832]{0:T(1024)} %reshape.361) | data formatting | bytes 18886656 | tf_op jit(solution)/shard_map/reshape | solution.py:74
  188.5 6.5 slice.169
  195.0 51.0 %rev.14 = f32[3,512,1024]{2,1,0:T(8,128)} reverse(f32[3,512,1024]{2,1,0:T(8,128)} %slice.169), dimensions={2} | reverse | bytes 12582912 | tf_op jit(solution)/shard_map/rev | solution.py:75
  246.1 9.4 all_gather.62
  255.5 8.7 all_gather.60
  264.2 9.4 all_gather.61
  273.6 8.7 all_gather.59
  287.0 4.4 fusion.75
  301.5 35.8 %reduce-scatter.27.cloned.1.call-done = bf16[256,768]{1,0:T(8,128)(2,1)} async-done(((bf16[1024,768]{1,0:T(8,128)(2,1)}), bf16[256,768]{1,0:T(8,128)(2,1)}) %reduce-scatter.27.cloned.1.call-update) | async-done | bytes 393232 | tf_op jit(solution)/shard_map/reduce_scatter | solution.py:54
  340.7 10.6 all_gather.68
  351.2 9.9 all_gather.66
  361.1 8.7 all_gather.67
  369.8 9.5 all_gather.64
  379.3 17.8 %all_gather.63 = bf16[512,768]{1,0:T(8,128)(2,1)S(1)} all-gather(bf16[128,768]{1,0:T(8,128)(2,1)S(1)} %copy-done.74), channel_id=1, replica_groups=mesh['dp'=8,'tensor'=4] {'tensor'}, dimensions={0}, use_global_device_ids=true | all-gather | bytes 983040 | tf_op jit(solution)/shard_map/all_gather | solution.py:238
  408.8 34.2 %reduce-scatter.29.cloned.1.call-done = bf16[256,768]{1,0:T(8,128)(2,1)} async-done(((bf16[1024,768]{1,0:T(8,128)(2,1)}), bf16[256,768]{1,0:T(8,128)(2,1)}) %reduce-scatter.29.cloned.1.call-update) | async-done | bytes 393232 | tf_op jit(solution)/shard_map/reduce_scatter | solution.py:54
  447.2 12.3 %all_gather.70 = bf16[768,512]{1,0:T(8,128)(2,1)} all-gather(bf16[96,512]{1,0:T(8,128)(2,1)} %param.35), channel_id=1, replica_groups=mesh['dp'=8,'tensor'=4] {'dp'}, dimensions={0}, use_global_device_ids=true | all-gather | bytes 884736 | tf_op jit(solution)/shard_map/all_gather | solution.py:183
  459.5 11.7 all_gather.71
  471.2 11.9 all_gather.72
  483.1 4.0 fusion.80
  489.5 30.5 %all-gather.14.cloned.1.call-done = bf16[1024,768]{1,0:T(8,128)(2,1)} async-done(((bf16[256,768]{1,0:T(8,128)(2,1)}), bf16[1024,768]{1,0:T(8,128)(2,1)}) %all-gather.14.cloned.1.call-update) | async-done | bytes 1572880 | tf_op jit(solution)/shard_map/all_gather | solution.py:50
  519.9 6.4 multiply_convert_fusion.4
  530.3 34.4 %reduce-scatter.33.cloned.1.call-done = bf16[256,768]{1,0:T(8,128)(2,1)} async-done(((bf16[1024,768]{1,0:T(8,128)(2,1)}), bf16[256,768]{1,0:T(8,128)(2,1)}) %reduce-scatter.33.cloned.1.call-update) | async-done | bytes 393232 | tf_op jit(solution)/shard_map/reduce_scatter | solution.py:54
  570.1 36.0 %all-gather.16.cloned.1.call-done = bf16[1024,768]{1,0:T(8,128)(2,1)} async-done(((bf16[256,768]{1,0:T(8,128)(2,1)}), bf16[1024,768]{1,0:T(8,128)(2,1)}) %all-gather.16.cloned.1.call-update) | async-done | bytes 1572880 | tf_op jit(solution)/shard_map/all_gather | solution.py:50
  618.0 3.7 convolution_convert_fusion
  621.7 30.6 %reduce-scatter.35.cloned.1.call-done = bf16[256,768]{1,0:T(8,128)(2,1)} async-done(((bf16[1024,768]{1,0:T(8,128)(2,1)}), bf16[256,768]{1,0:T(8,128)(2,1)}) %reduce-scatter.35.cloned.1.call-update) | async-done | bytes 393232 | tf_op jit(solution)/shard_map/reduce_scatter | solution.py:54
  655.0 33.9 %reduce-scatter.31.cloned.1.call-done = bf16[256,768]{1,0:T(8,128)(2,1)} async-done(((bf16[1024,768]{1,0:T(8,128)(2,1)}), bf16[256,768]{1,0:T(8,128)(2,1)}) %reduce-scatter.31.cloned.1.call-update) | async-done | bytes 393232 | tf_op jit(solution)/shard_map/reduce_scatter | solution.py:54
  688.8 3.5 fusion.68
  708.4 20.0 %all-gather.18.cloned.1.call-done = bf16[1024,768]{1,0:T(8,128)(2,1)} async-done(((bf16[256,768]{1,0:T(8,128)(2,1)}), bf16[1024,768]{1,0:T(8,128)(2,1)}) %all-gather.18.cloned.1.call-update) | async-done | bytes 1572880 | tf_op jit(solution)/shard_map/all_gather | solution.py:50
  730.5 3.9 multiply_reduce_fusion
  748.8 3.4 fusion.82
  758.4 4.2 fusion.14
  765.2 3.9 fusion.93
  769.2 3.9 fusion.91
  773.1 3.9 fusion.92
  797.5 34.9 %rev.17 = f32[3,512,1024]{2,1,0:T(8,128)} reverse(bf16[3,512,1024]{2,1,0:T(8,128)(2,1)S(1)} %multiply_convert_fusion), dimensions={2} | reverse | bytes 9437184 | tf_op jit(solution)/shard_map/rev | solution.py:80
  832.3 48.0 %rev.16 = f32[3,512,1024]{2,1,0:T(8,128)} reverse(bf16[3,512,1024]{2,1,0:T(8,128)(2,1)} %copy-done.9), dimensions={2} | reverse | bytes 9437184 | tf_op jit(solution)/shard_map/rev | solution.py:80
  880.4 7.7 pad.24
  888.1 16.2 %reshape.365 = f32[2360832]{0:T(1024)} reshape(f32[3,512,1537]{2,1,0:T(8,128)} %pad.24) | data formatting | bytes 18886656
  904.3 13.3 %reshape.341 = f32[3,786944]{1,0:T(4,128)} reshape(f32[2360832]{0:T(1024)} %reshape.365) | data formatting | bytes 18886656 | tf_op jit(solution)/shard_map/reshape | solution.py:82
  917.5 10.5 pad.25
  928.0 15.5 %reshape.342 = f32[3,513,1536]{2,1,0:T(8,128)} reshape(f32[3,787968]{1,0:T(4,128)} %pad.25) | data formatting | bytes 18911232 | tf_op jit(solution)/shard_map/reshape | solution.py:84
  943.5 4.3 reduce_sum.185
  947.8 7.7 pad.26
  955.5 16.4 %reshape.363 = f32[2360832]{0:T(1024)} reshape(f32[3,512,1537]{2,1,0:T(8,128)} %pad.26) | data formatting | bytes 18886656
  971.9 13.4 %reshape.343 = f32[3,786944]{1,0:T(4,128)} reshape(f32[2360832]{0:T(1024)} %reshape.363) | data formatting | bytes 18886656 | tf_op jit(solution)/shard_map/reshape | solution.py:82
  985.3 10.2 pad.27
  995.5 15.2 %reshape.344 = f32[3,513,1536]{2,1,0:T(8,128)} reshape(f32[3,787968]{1,0:T(4,128)} %pad.27) | data formatting | bytes 18911232 | tf_op jit(solution)/shard_map/reshape | solution.py:84
  1010.7 4.4 reduce_sum.186
  1023.0 39.3 %all-reduce.6 = (f32[32,12]{0,1:T(8,128)S(1)}, f32[3,768]{1,0:T(4,128)S(1)}) all-reduce(f32[32,12]{0,1:T(8,128)S(1)} %dynamic_update_slice.3, f32[3,768]{1,0:T(4,128)S(1)} %pad_maximum_fusion.4), channel_id=1, replica_groups=mesh['dp'=8,'tensor'=4] {'dp','tensor'}, use_global_device_ids=true, to_apply=%region_40.41 | all-reduce | flops 2688 | bytes 21504 | tf_op jit(solution)/shard_map/psum | solution.py:361
  1068.4 38.7 %reduce-scatter.57.cloned.1.call-done = f32[96,192]{1,0:T(8,128)} async-done(((f32[768,192]{1,0:T(8,128)}), f32[96,192]{1,0:T(8,128)}) %reduce-scatter.57.cloned.1.call-update) | async-done | bytes 73744
  1107.1 38.7 %reduce-scatter.45.cloned.1.call-done = f32[96,192]{1,0:T(8,128)} async-done(((f32[768,192]{1,0:T(8,128)}), f32[96,192]{1,0:T(8,128)}) %reduce-scatter.45.cloned.1.call-update) | async-done | bytes 73744 | tf_op jit(solution)/shard_map/reduce_scatter | solution.py:368
  1145.8 38.7 %reduce-scatter.41.cloned.1.call-done = f32[96,192]{1,0:T(8,128)} async-done(((f32[768,192]{1,0:T(8,128)}), f32[96,192]{1,0:T(8,128)}) %reduce-scatter.41.cloned.1.call-update) | async-done | bytes 73744 | tf_op jit(solution)/shard_map/reduce_scatter | solution.py:366
  1184.5 38.5 %reduce-scatter.43.cloned.1.call-done = f32[96,192]{1,0:T(8,128)} async-done(((f32[768,192]{1,0:T(8,128)}), f32[96,192]{1,0:T(8,128)}) %reduce-scatter.43.cloned.1.call-update) | async-done | bytes 73744 | tf_op jit(solution)/shard_map/reduce_scatter | solution.py:367
  (384 shorter events, 139.9 us)
Async XLA Ops:
  7.2 13.9 %copy-start = (bf16[32,3]{0,1:T(4,128)(2,1)S(1)}, bf16[32,3]{0,1:T(4,128)(2,1)}, u32[]{:S(2)}) copy-start(bf16[32,3]{0,1:T(4,128)(2,1)} %param.38) | copy-start | bytes 580
  7.2 276.8 %all-gather.8.cloned.1.call-start = ((), (), s32[]{:S(2)}) async-start(), calls=%async_computation.18 | async-start | bytes 1966080 | tf_op jit(solution)/shard_map/all_gather | solution.py:50
  8.4 13.5 %copy-start.87 = (f32[256]{0:T(256)}, f32[256]{0:T(256)S(1)}, u32[]{:S(2)}) copy-start(f32[256]{0:T(256)S(1)} %add_rsqrt_fusion.2) | copy-start | bytes 3076
  19.1 319.4 %copy-start.77 = (f32[768]{0:T(1024)}, f32[768]{0:T(1024)S(1)}, u32[]{:S(2)}) copy-start(f32[768]{0:T(1024)S(1)} %get-tuple-element.110) | copy-start | bytes 9220
  21.1 316.2 %reduce-scatter.27.cloned.1.call-start = ((), (), s32[]{:S(2)}) async-start(), calls=%async_computation.19 | async-start | bytes 1966080 | tf_op jit(solution)/shard_map/reduce_scatter | solution.py:54
  195.0 60.5 %copy-start.79 = (bf16[96,192]{1,0:T(8,128)(2,1)S(1)}, bf16[96,192]{1,0:T(8,128)(2,1)}, u32[]{:S(2)}) copy-start(bf16[96,192]{1,0:T(8,128)(2,1)} %param.27) | copy-start | bytes 110596
  195.0 69.2 %copy-start.80 = (bf16[96,192]{1,0:T(8,128)(2,1)S(1)}, bf16[96,192]{1,0:T(8,128)(2,1)}, u32[]{:S(2)}) copy-start(bf16[96,192]{1,0:T(8,128)(2,1)} %param.28) | copy-start | bytes 110596
  195.0 78.6 %copy-start.81 = (bf16[96,192]{1,0:T(8,128)(2,1)S(1)}, bf16[96,192]{1,0:T(8,128)(2,1)}, u32[]{:S(2)}) copy-start(bf16[96,192]{1,0:T(8,128)(2,1)} %param.29) | copy-start | bytes 110596
  195.0 87.3 %copy-start.91 = (s32[1,1024]{1,0:T(1,128)S(1)}, s32[1,1024]{1,0:T(1,128)}, u32[]{:S(2)}) copy-start(s32[1,1024]{1,0:T(1,128)} %param.24) | copy-start | bytes 12292
  255.5 43.3 %copy-start.30 = (bf16[192,768]{0,1:T(8,128)(2,1)}, bf16[192,768]{0,1:T(8,128)(2,1)S(1)}, u32[]{:S(2)}) copy-start(bf16[192,768]{0,1:T(8,128)(2,1)S(1)} %all_gather.62) | copy-start | bytes 884740
  264.2 22.0 %copy-start.44 = (bf16[768,192]{1,0:T(8,128)(2,1)}, bf16[768,192]{1,0:T(8,128)(2,1)S(1)}, u32[]{:S(2)}) copy-start(bf16[768,192]{1,0:T(8,128)(2,1)S(1)} %all_gather.60) | copy-start | bytes 884740
  273.6 13.3 %copy-start.43 = (bf16[768,192]{1,0:T(8,128)(2,1)}, bf16[768,192]{1,0:T(8,128)(2,1)S(1)}, u32[]{:S(2)}) copy-start(bf16[768,192]{1,0:T(8,128)(2,1)S(1)} %all_gather.61) | copy-start | bytes 884740
  282.4 13.4 %copy-start.28 = (bf16[768,192]{1,0:T(8,128)(2,1)}, bf16[768,192]{1,0:T(8,128)(2,1)S(1)}, u32[]{:S(2)}) copy-start(bf16[768,192]{1,0:T(8,128)(2,1)S(1)} %all_gather.59) | copy-start | bytes 884740
  286.2 6.6 copy-start.55
  286.9 5.9 copy-start.15
  287.0 5.9 slice-start.6
  287.0 5.9 slice-start.7
  298.8 38.5 %copy-start.8 = (bf16[256,768]{1,0:T(8,128)(2,1)S(1)}, bf16[256,768]{1,0:T(8,128)(2,1)}, u32[]{:S(2)}) copy-start(bf16[256,768]{1,0:T(8,128)(2,1)} %param.22) | copy-start | bytes 1179652
  299.6 40.9 %copy-start.85 = (bf16[192,96]{1,0:T(8,128)(2,1)S(1)}, bf16[192,96]{1,0:T(8,128)(2,1)}, u32[]{:S(2)}) copy-start(bf16[192,96]{1,0:T(8,128)(2,1)} %param.34) | copy-start | bytes 110596
  299.6 51.6 %copy-start.82 = (bf16[96,192]{1,0:T(8,128)(2,1)S(1)}, bf16[96,192]{1,0:T(8,128)(2,1)}, u32[]{:S(2)}) copy-start(bf16[96,192]{1,0:T(8,128)(2,1)} %param.31) | copy-start | bytes 110596
  299.6 61.5 %copy-start.83 = (bf16[96,192]{1,0:T(8,128)(2,1)S(1)}, bf16[96,192]{1,0:T(8,128)(2,1)}, u32[]{:S(2)}) copy-start(bf16[96,192]{1,0:T(8,128)(2,1)} %param.32) | copy-start | bytes 110596
  301.4 68.4 %copy-start.84 = (bf16[96,192]{1,0:T(8,128)(2,1)S(1)}, bf16[96,192]{1,0:T(8,128)(2,1)}, u32[]{:S(2)}) copy-start(bf16[96,192]{1,0:T(8,128)(2,1)} %param.33) | copy-start | bytes 110596
  301.4 77.9 %copy-start.74 = (bf16[128,768]{1,0:T(8,128)(2,1)S(1)}, bf16[128,768]{1,0:T(8,128)(2,1)}, u32[]{:S(2)}) copy-start(bf16[128,768]{1,0:T(8,128)(2,1)} %param.23) | copy-start | bytes 589828
  301.4 97.8 %all-gather.10.cloned.1.call-start = ((), (), s32[]{:S(2)}) async-start(), calls=%async_computation.20 | async-start | bytes 1966080 | tf_op jit(solution)/shard_map/all_gather | solution.py:50
  338.5 60.7 %copy-start.92 = (f32[256]{0:T(256)}, f32[256]{0:T(256)S(1)}, u32[]{:S(2)}) copy-start(f32[256]{0:T(256)S(1)} %add_rsqrt_fusion.1) | copy-start | bytes 3076
  340.5 102.5 %reduce-scatter.29.cloned.1.call-start = ((), (), s32[]{:S(2)}) async-start(), calls=%async_computation.21 | async-start | bytes 1966080 | tf_op jit(solution)/shard_map/reduce_scatter | solution.py:54
  361.1 40.2 %copy-start.32 = (bf16[768,192]{1,0:T(8,128)(2,1)}, bf16[768,192]{1,0:T(8,128)(2,1)S(1)}, u32[]{:S(2)}) copy-start(bf16[768,192]{1,0:T(8,128)(2,1)S(1)} %all_gather.66) | copy-start | bytes 884740
  369.8 27.2 %copy-start.42 = (bf16[768,192]{1,0:T(8,128)(2,1)}, bf16[768,192]{1,0:T(8,128)(2,1)S(1)}, u32[]{:S(2)}) copy-start(bf16[768,192]{1,0:T(8,128)(2,1)S(1)} %all_gather.67) | copy-start | bytes 884740
  379.3 18.9 %copy-start.40 = (bf16[768,192]{1,0:T(8,128)(2,1)}, bf16[768,192]{1,0:T(8,128)(2,1)S(1)}, u32[]{:S(2)}) copy-start(bf16[768,192]{1,0:T(8,128)(2,1)S(1)} %all_gather.64) | copy-start | bytes 884740
  408.8 74.3 %all-gather.12.cloned.1.call-start = ((), (), s32[]{:S(2)}) async-start(), calls=%async_computation.22 | async-start | bytes 1966080 | tf_op jit(solution)/shard_map/all_gather | solution.py:50
  444.4 122.5 %copy-start.86 = (f32[256]{0:T(256)}, f32[256]{0:T(256)S(1)}, u32[]{:S(2)}) copy-start(f32[256]{0:T(256)S(1)} %add_rsqrt_fusion) | copy-start | bytes 3076
  446.5 73.4 %all-gather.14.cloned.1.call-start = ((), (), s32[]{:S(2)}) async-start(), calls=%async_computation.24 | async-start | bytes 1966080 | tf_op jit(solution)/shard_map/all_gather | solution.py:50
  447.1 117.6 %reduce-scatter.33.cloned.1.call-start = ((), (), s32[]{:S(2)}) async-start(), calls=%async_computation.25 | async-start | bytes 1966080 | tf_op jit(solution)/shard_map/reduce_scatter | solution.py:54
  519.9 6.4 copy-start.49
  530.3 75.8 %all-gather.16.cloned.1.call-start = ((), (), s32[]{:S(2)}) async-start(), calls=%async_computation.26 | async-start | bytes 1966080 | tf_op jit(solution)/shard_map/all_gather | solution.py:50
  570.0 82.3 %reduce-scatter.35.cloned.1.call-start = ((), (), s32[]{:S(2)}) async-start(), calls=%async_computation.27 | async-start | bytes 1966080 | tf_op jit(solution)/shard_map/reduce_scatter | solution.py:54
  617.9 34.5 %copy-start.78 = (f32[768]{0:T(1024)S(1)}, f32[768]{0:T(1024)}, u32[]{:S(2)}) copy-start(f32[768]{0:T(1024)} %copy-done.77) | copy-start | bytes 9220
  617.9 70.9 %reduce-scatter.31.cloned.1.call-start = ((), (), s32[]{:S(2)}) async-start(), calls=%async_computation.23 | async-start | bytes 1966080 | tf_op jit(solution)/shard_map/reduce_scatter | solution.py:54
  621.7 106.7 %all-gather.18.cloned.1.call-start = ((), (), s32[]{:S(2)}) async-start(), calls=%async_computation.28 | async-start | bytes 1966080 | tf_op jit(solution)/shard_map/all_gather | solution.py:50
  692.4 101.8 %reduce-scatter.61.cloned.1.call-start = ((), (), s32[]{:S(2)}) async-start(), calls=%async_computation.41 | async-start | bytes 884736
  702.5 93.2 %reduce-scatter.39.cloned.1.call-start = ((), (), s32[]{:S(2)}) async-start(), calls=%async_computation.30 | async-start | bytes 983040 | tf_op jit(solution)/shard_map/reduce_scatter | solution.py:311
  705.9 22.5 %copy-start.31 = (bf16[192,768]{0,1:T(8,128)(2,1)S(1)}, bf16[192,768]{0,1:T(8,128)(2,1)}, u32[]{:S(2)}) copy-start(bf16[192,768]{0,1:T(8,128)(2,1)} %copy-done.30) | copy-start | bytes 884740
  706.6 23.9 %copy-start.18 = (bf16[1024,192]{0,1:T(8,128)(2,1)S(1)}, bf16[1024,192]{0,1:T(8,128)(2,1)}, u32[]{:S(2)}) copy-start(bf16[1024,192]{0,1:T(8,128)(2,1)} %copy-done.17) | copy-start | bytes 1179652
  707.9 312.1 %reduce-scatter.55.cloned.1.call-start = ((), (), s32[]{:S(2)}) async-start(), calls=%async_computation.38 | async-start | bytes 884736
  730.5 8.0 copy-start.63
  746.8 5.4 copy-start.10
  746.8 5.4 copy-start.56
  748.8 5.5 slice-start.4
  756.4 265.2 %reduce-scatter.37.cloned.1.call-start = ((), (), s32[]{:S(2)}) async-start(), calls=%async_computation.29 | async-start | bytes 1966080 | tf_op jit(solution)/shard_map/reduce_scatter | solution.py:54
  765.2 300.6 %reduce-scatter.53.cloned.1.call-start = ((), (), s32[]{:S(2)}) async-start(), calls=%async_computation.37 | async-start | bytes 1769472 | tf_op jit(solution)/shard_map/reduce_scatter | solution.py:376
  769.1 296.6 %reduce-scatter.49.cloned.1.call-start = ((), (), s32[]{:S(2)}) async-start(), calls=%async_computation.35 | async-start | bytes 1769472 | tf_op jit(solution)/shard_map/reduce_scatter | solution.py:374
  773.1 292.6 %reduce-scatter.51.cloned.1.call-start = ((), (), s32[]{:S(2)}) async-start(), calls=%async_computation.36 | async-start | bytes 1769472 | tf_op jit(solution)/shard_map/reduce_scatter | solution.py:375
  777.0 288.7 %reduce-scatter.59.cloned.1.call-start = ((), (), s32[]{:S(2)}) async-start(), calls=%async_computation.40 | async-start | bytes 884736
  781.8 286.7 %reduce-scatter.47.cloned.1.call-start = ((), (), s32[]{:S(2)}) async-start(), calls=%async_computation.34 | async-start | bytes 884736 | tf_op jit(solution)/shard_map/reduce_scatter | solution.py:370
  784.8 322.3 %reduce-scatter.57.cloned.1.call-start = ((), (), s32[]{:S(2)}) async-start(), calls=%async_computation.39 | async-start | bytes 884736
  787.3 6.9 copy-start.89
  787.3 10.2 copy-start.90
  789.6 356.3 %reduce-scatter.45.cloned.1.call-start = ((), (), s32[]{:S(2)}) async-start(), calls=%async_computation.33 | async-start | bytes 884736 | tf_op jit(solution)/shard_map/reduce_scatter | solution.py:368
  792.6 391.9 %reduce-scatter.41.cloned.1.call-start = ((), (), s32[]{:S(2)}) async-start(), calls=%async_computation.31 | async-start | bytes 884736 | tf_op jit(solution)/shard_map/reduce_scatter | solution.py:366
  1015.2 6.5 copy-start.76
  1015.2 6.5 copy-start.88
  1016.7 46.8 %copy-start.50 = (f32[256,768]{1,0:T(8,128)S(1)}, f32[256,768]{1,0:T(8,128)}, u32[]{:S(2)}) copy-start(f32[256,768]{1,0:T(8,128)} %get-tuple-element.116) | copy-start | bytes 2359300
  1016.7 206.3 %reduce-scatter.43.cloned.1.call-start = ((), (), s32[]{:S(2)}) async-start(), calls=%async_computation.32 | async-start | bytes 884736 | tf_op jit(solution)/shard_map/reduce_scatter | solution.py:367
  1017.5 205.6 %copy-start.1 = (bf16[32,3]{0,1:T(4,128)(2,1)S(1)}, bf16[32,3]{0,1:T(4,128)(2,1)}, u32[]{:S(2)}) copy-start(bf16[32,3]{0,1:T(4,128)(2,1)} %param.38) | copy-start | bytes 580
  (64 other events, 155.7 us)
Sparse Core Ops, SparseCore 0:
  21.2 37.1 all-gather.7
  301.5 35.6 reduce-scatter.26
  340.6 35.8 all-gather.9
  408.9 34.1 reduce-scatter.28
  446.7 35.8 all-gather.11
  484.0 35.8 all-gather.13
  530.4 34.2 reduce-scatter.32
  570.2 35.8 all-gather.15
  618.0 34.2 reduce-scatter.34
  654.5 34.2 reduce-scatter.30
  692.5 35.8 all-gather.17
  731.4 33.8 reduce-scatter.60
  767.5 23.1 reduce-scatter.38
  793.7 34.5 reduce-scatter.54
  830.5 35.4 reduce-scatter.36
  869.7 37.2 reduce-scatter.52
  910.7 38.3 reduce-scatter.48
  952.8 38.3 reduce-scatter.50
  994.9 34.9 reduce-scatter.58
  1033.4 34.9 reduce-scatter.46
  1072.2 34.9 reduce-scatter.56
  1110.9 34.9 reduce-scatter.44
  1149.6 34.9 reduce-scatter.40
  1188.1 34.9 reduce-scatter.42
where the time goes:
time: 1250 us; the launch traced here: 1230 us
  local copies, waits for them, and re-layouts  454 us (36%)
  waiting for transfers between devices  414 us (33%)
  blocking collectives  178 us (14%)
  matrix products  119 us (10%)
  other arithmetic  47.5 us (4%)
  between operations  15.9 us (1%)
    reduce_scatter x6, waiting for transfers between devices, scatter_rows(): lax.psum_scatter(term(jnp.int32(0), lax.axis_size('tensor') * count).asty...  169 us
    unnamed x221, local copies, waits for them, and re-layouts  118 us
    rev x2, local copies, waits for them, and re-layouts, skewed_grid(): return grid[:, :, ::-1]  102 us
    all_gather x6, waiting for transfers between devices, gather_rows(): return lax.all_gather(value, 'tensor', axis=0, tiled=True)  86.4 us
    rev x2, local copies, waits for them, and re-layouts, diagonal_sums(): flipped = grid[:, :, ::-1]  82.9 us
    unnamed x28, waiting for transfers between devices  39.7 us
    psum x1, blocking collectives, per_device(): gain_sum, table_sum = lax.psum((gain_grads, table_full), ('dp', 'tensor'))  39.3 us
    reduce_scatter x1, waiting for transfers between devices, per_device(): lax.psum_scatter(grad_self_query, 'dp', scatter_dimension=0, tiled=True)  38.7 us
  transfers between devices with their start and end apart: 24, of which 13 were waited for; matrix products, arithmetic and copies ran while one was open for 45% of the time, Pallas kernels for 0%

commit v1 on v0

v1 whole, which is shorter than its diff:
```python
from functools import partial

import jax
import jax.numpy as jnp
from jax import lax
from jax.experimental import pallas as pl
from jax.experimental.pallas import tpu as pltpu
from jax.sharding import PartitionSpec as P

DK = 64
EPS = 1e-06
MASKED = -1e30
BF = jnp.bfloat16
F32 = jnp.float32
MESH = pl.DeviceIdType.MESH
VMEM = pl.BlockSpec(memory_space=pltpu.VMEM)
ANY = pl.BlockSpec(memory_space=pl.ANY)
LIMIT = 62 * 1024 * 1024
STEP = 256


def dot(a, b):
    return jnp.dot(a, b, preferred_element_type=F32)


def dot_nt(a, b):
    return lax.dot_general(a, b, (((1,), (1,)), ((), ())), preferred_element_type=F32)


def dot_tn(a, b):
    return lax.dot_general(a, b, (((0,), (0,)), ((), ())), preferred_element_type=F32)


def norm_scale(x):
    return lax.rsqrt(jnp.mean(x * x, axis=-1, keepdims=True) + EPS)


def norm_back(x, r, g, u):
    w = u * g
    inner = jnp.mean(w * x, axis=-1, keepdims=True)
    return r * w - x * (r * r * r * inner), jnp.sum(u * (x * r), axis=0, keepdims=True)


def flip(index, bit):
    size = 1 << bit
    return index + size - 2 * size * lax.rem(index // size, 2)


def flip_all(index, mask):
    bit = 0
    while mask:
        if mask & 1:
            index = flip(index, bit)
        mask >>= 1
        bit += 1
    return index


def subsets(bits):
    out = [0]
    for b in bits:
        out = out + [m | (1 << b) for m in out]
    return out


def bit_orders(count):
    upper = list(range(1, count))
    return [upper + [0], upper[::-1] + [0]]


class Sems:
    def __init__(self, ref):
        self.ref = ref
        self.used = 0

    def take(self):
        self.used += 1
        return self.ref.at[self.used - 1]


def wait_bytes(ref, sem):
    pltpu.make_async_copy(ref, ref, sem).wait()


def enter(nt, nd):
    me_t, me_d = lax.axis_index("tensor"), lax.axis_index("dp")
    bar = pltpu.get_barrier_semaphore()
    bits = nd.bit_length() - 1
    for b in range(bits):
        pl.semaphore_signal(bar, 1, device_id={"dp": flip(me_d, b)}, device_id_type=MESH)

    @pl.when(me_t > 0)
    def _():
        pl.semaphore_signal(bar, 1, device_id={"tensor": me_t - 1}, device_id_type=MESH)

    @pl.when(me_t < nt - 1)
    def _():
        pl.semaphore_signal(bar, 1, device_id={"tensor": me_t + 1}, device_id_type=MESH)

    pl.semaphore_wait(bar, bits + (me_t + nt - 1) // nt + (2 * nt - 2 - me_t) // nt)
    return me_t, me_d


def run_jobs(jobs, after):
    last = max(start + len(stages) for start, stages in jobs)
    for tick in range(last):
        for start, stages in jobs:
            if 0 <= tick - start < len(stages):
                stages[tick - start]()
    for fn in after:
        fn()


def line_gather(nt, me, own, slot, sends, recvs, after):
    sem = {(s, j): (sends.take(), recvs.take()) for s in (1, -1) for j in range(1, nt)}

    def send(side, j):
        block = me - side * (j - 1)
        target = me + side
        ok = (block >= 0) & (block < nt) & (target >= 0) & (target < nt)
        src = own if j == 1 else slot(jnp.clip(block, 0, nt - 1))
        dst = slot(jnp.clip(block, 0, nt - 1))
        ss, rs = sem[side, j]

        @pl.when(ok)
        def _():
            pltpu.make_async_remote_copy(
                src, dst, ss, rs, device_id={"tensor": target}, device_id_type=MESH
            ).start()

        def done():
            @pl.when(ok)
            def _():
                wait_bytes(own, ss)

        after.append(done)

    def arrive(side, j):
        block = me - side * j

        @pl.when((block >= 0) & (block < nt))
        def _():
            wait_bytes(own, sem[side, j][1])

    def stage(j):
        def run():
            for side in (1, -1):
                if j > 0:
                    arrive(side, j)
                if j < nt - 1:
                    send(side, j + 1)

        return run

    return [stage(j) for j in range(nt)]


def cube_gather(nd, me, order, own, slot, slots, sends, recvs, after):
    count = len(order)
    sem = [(sends.take(), recvs.take()) for _ in range(count)]

    def start(k):
        bit = order[k]
        for m in subsets(order[:k]):
            block = flip_all(me, m)
            src = own if (m == 0 and own is not None) else slot(block)
            pltpu.make_async_remote_copy(
                src, slot(block), sem[k][0], sem[k][1], device_id={"dp": flip(me, bit)}, device_id_type=MESH
            ).start()

        def done():
            wait_bytes(slots(1 << k), sem[k][0])

        after.append(done)

    def stage(k):
        def run():
            if k > 0:
                wait_bytes(slots(1 << (k - 1)), sem[k - 1][1])
            if k < count:
                start(k)

        return run

    return [stage(k) for k in range(count + 1)]


def gather_kernel(
    nt, nd, tok_ref, enc_ref, wa_ref, wb_ref, tok_out, enc_out, wa_out, wb_out, ssem, rsem, lsem
):
    me_t, me_d = enter(nt, nd)
    bits = nd.bit_length() - 1
    sends, recvs, after = Sems(ssem), Sems(rsem), []
    locals_ = [
        (tok_ref, tok_out.at[me_t]),
        (enc_ref, enc_out.at[me_t]),
        (wa_ref, wa_out.at[me_d]),
        (wb_ref, wb_out.at[me_t, me_d]),
    ]
    for n, (src, dst) in enumerate(locals_):
        pltpu.make_async_copy(src, dst, lsem.at[n]).start()
    orders = bit_orders(bits)
    cols = wb_ref.shape[1]
    chunks = cols // STEP
    half = STEP // 2
    jobs = []
    jobs.append(
        (0, cube_gather(nd, me_d, orders[0], wa_ref, lambda d: wa_out.at[d], lambda n: wa_out.at[pl.ds(0, n)], sends, recvs, after))
    )

    def chunk_job(c):
        first = c * STEP
        z = line_gather(
            nt,
            me_t,
            wb_ref.at[:, pl.ds(first, STEP)],
            lambda t: wb_out.at[t, me_d, :, pl.ds(first, STEP)],
            sends,
            recvs,
            after,
        )
        cubes = []
        for n in range(2):
            at = first + n * half
            cubes.append(
                cube_gather(
                    nd,
                    me_d,
                    orders[n],
                    None,
                    lambda d, at=at: wb_out.at[:, d, :, pl.ds(at, half)],
                    lambda k, at=at: wb_out.at[:, pl.ds(0, k), :, pl.ds(at, half)],
                    sends,
                    recvs,
                    after,
                )
            )

        def meet():
            z[-1]()
            for q in cubes:
                q[0]()

        def both(k):
            def run():
                for q in cubes:
                    q[k]()

            return run

        return z[:-1] + [meet] + [both(k) for k in range(1, bits + 1)]

    tok_job = line_gather(nt, me_t, tok_ref, lambda t: tok_out.at[t], sends, recvs, after)
    enc_job = line_gather(nt, me_t, enc_ref, lambda t: enc_out.at[t], sends, recvs, after)
    for c in range(chunks):
        jobs.append((c, chunk_job(c)))
    jobs.append((2, tok_job))
    jobs.append((5, enc_job))
    pltpu.make_async_copy(wb_ref, wb_out.at[me_t, me_d], lsem.at[3]).wait()
    for n in range(3):
        src, dst = locals_[n]
        after.append(lambda n=n, src=src, dst=dst: pltpu.make_async_copy(src, dst, lsem.at[n]).wait())
    run_jobs(jobs, after)


def gather_all(nt, nd, tok, enc, wa, wb):
    bits = nd.bit_length() - 1
    chunks = wb.shape[1] // STEP
    total = (chunks + 2) * 2 * (nt - 1) + (2 * chunks + 1) * bits
    return pl.pallas_call(
        partial(gather_kernel, nt, nd),
        out_shape=(
            jax.ShapeDtypeStruct((nt,) + tok.shape, BF),
            jax.ShapeDtypeStruct((nt,) + enc.shape, BF),
            jax.ShapeDtypeStruct((nd,) + wa.shape, BF),
            jax.ShapeDtypeStruct((nt, nd) + wb.shape, BF),
        ),
        in_specs=[VMEM] * 4,
        out_specs=(ANY,) * 4,
        scratch_shapes=[
            pltpu.SemaphoreType.DMA((total,)),
            pltpu.SemaphoreType.DMA((total,)),
            pltpu.SemaphoreType.DMA((4,)),
        ],
        compiler_params=pltpu.CompilerParams(collective_id=0, has_side_effects=True),
        name="gather_all",
    )(tok, enc, wa, wb)


def exchange_kernel(nt, x_ref, o_ref, ssem, rsem, lsem):
    me = lax.axis_index("tensor")
    bar = pltpu.get_barrier_semaphore()
    for k in range(1, nt):
        pl.semaphore_signal(bar, 1, device_id={"tensor": lax.rem(me + k, nt)}, device_id_type=MESH)
    pl.semaphore_wait(bar, nt - 1)
    local = pltpu.make_async_copy(x_ref.at[me], o_ref.at[me], lsem)
    local.start()
    copies = []
    for k in range(1, nt):
        peer = lax.rem(me + k, nt)
        copy = pltpu.make_async_remote_copy(
            x_ref.at[peer], o_ref.at[me], ssem.at[k], rsem.at[k], device_id={"tensor": peer}, device_id_type=MESH
        )
        copy.start()
        copies.append(copy)
    local.wait()
    for copy in copies:
        copy.wait()


def exchange(nt, x, ident):
    return pl.pallas_call(
        partial(exchange_kernel, nt),
        out_shape=jax.ShapeDtypeStruct(x.shape, x.dtype),
        in_specs=[VMEM],
        out_specs=VMEM,
        scratch_shapes=[
            pltpu.SemaphoreType.DMA((nt,)),
            pltpu.SemaphoreType.DMA((nt,)),
            pltpu.SemaphoreType.DMA,
        ],
        compiler_params=pltpu.CompilerParams(collective_id=ident, has_side_effects=True),
        name="exchange",
    )(x)


def cube_scatter(nd, me, order, value, recv, sends, recvs, after):
    count = len(order)
    sem = [(sends.take(), recvs.take()) for _ in range(count)]

    def start(k):
        bit = order[k]
        peer = flip(me, bit)
        for j, m in enumerate(subsets(order[k + 1 :])):
            pltpu.make_async_remote_copy(
                value(flip_all(peer, m)),
                recv[k].at[j],
                sem[k][0],
                sem[k][1],
                device_id={"dp": peer},
                device_id_type=MESH,
            ).start()

        def done():
            wait_bytes(recv[k], sem[k][0])

        after.append(done)

    def land(k):
        wait_bytes(recv[k], sem[k][1])
        for j, m in enumerate(subsets(order[k + 1 :])):
            ref = value(flip_all(me, m))
            got = recv[k].at[j]
            if len(ref.shape) == 2:
                ref[...] = (ref[...].astype(F32) + got[...].astype(F32)).astype(BF)
            else:
                for t in range(ref.shape[0]):
                    ref[t] = (ref[t].astype(F32) + got[t].astype(F32)).astype(BF)

    def stage(k):
        def run():
            if k > 0:
                land(k - 1)
            if k < count:
                start(k)

        return run

    return [stage(k) for k in range(count + 1)]


def line_scatter(nt, me, value, recv, finish, sends, recvs, after):
    sem = {(s, b): (sends.take(), recvs.take()) for s in (0, 1) for b in range(nt)}

    def hop(z):
        def run():
            for side, here in ((0, z), (1, nt - 1 - z)):
                goal = here + 1 if side == 0 else here - 1
                blocks = range(here + 1, nt) if side == 0 else range(here - 1, -1, -1)

                @pl.when(me == here)
                def _(side=side, goal=goal, blocks=blocks):
                    for b in blocks:
                        ref = value(b)
                        if z > 0:
                            got = recv.at[side, b]
                            wait_bytes(got, sem[side, b][1])
                            ref[...] = (ref[...].astype(F32) + got[...].astype(F32)).astype(BF)
                        pltpu.make_async_remote_copy(
                            ref,
                            recv.at[side, b],
                            sem[side, b][0],
                            sem[side, b][1],
                            device_id={"tensor": goal},
                            device_id_type=MESH,
                        ).start()

        return run

    def last():
        for here in range(nt):

            @pl.when(me == here)
            def _(here=here):
                if here > 0:
                    wait_bytes(recv.at[0, here], sem[0, here][1])
                if here < nt - 1:
                    wait_bytes(recv.at[1, here], sem[1, here][1])
                total = value(here)[...].astype(F32)
                if here > 0:
                    total = total + recv[0, here].astype(F32)
                if here < nt - 1:
                    total = total + recv[1, here].astype(F32)
                finish(total)

    def done():
        for here in range(nt):

            @pl.when(me == here)
            def _(here=here):
                for b in range(here + 1, nt):
                    wait_bytes(recv.at[0, b], sem[0, b][0])
                for b in range(here):
                    wait_bytes(recv.at[1, b], sem[1, b][0])

    after.append(done)
    return [hop(z) for z in range(nt - 1)] + [last]


def scatter_kernel(
    nt,
    nd,
    g_ref,
    a_ref,
    u_ref,
    e_ref,
    gg_ref,
    tt_ref,
    g_out,
    a_out,
    u_out,
    e_out,
    *scratch,
):
    bits = nd.bit_length() - 1
    gv, uz, ez, gz = scratch[:4]
    arecv = scratch[4 : 4 + bits]
    grecv = scratch[4 + bits : 4 + 2 * bits]
    ssem, rsem, lsem = scratch[4 + 2 * bits :]
    cols = g_ref.shape[3]
    chunks = cols // STEP
    half = STEP // 2
    for c in range(chunks):
        at = pl.ds(c * STEP, STEP)
        pltpu.make_async_copy(g_ref.at[:, :, :, at], gv.at[:, :, :, at], lsem.at[c]).start()
    me_t, me_d = enter(nt, nd)
    sends, recvs, after = Sems(ssem), Sems(rsem), []
    orders = [[0] + o[:-1][::-1] for o in bit_orders(bits)]
    heads = tt_ref.shape[0]
    wide = a_ref.shape[2]
    for d in range(nd):
        a_ref[d, :heads, wide - 128 :] = tt_ref[...].astype(BF)
    jobs = []

    def a_done():
        a_out[...] = a_ref[me_d].astype(F32)

    a_job = cube_scatter(nd, me_d, orders[0], lambda d: a_ref.at[d], arecv, sends, recvs, after) + [a_done]

    def chunk_job(c):
        first = c * STEP
        cubes = []
        for n in range(2):
            at = first + n * half
            cubes.append(
                cube_scatter(
                    nd,
                    me_d,
                    orders[n],
                    lambda d, at=at: gv.at[:, d, :, pl.ds(at, half)],
                    [r.at[2 * c + n] for r in grecv],
                    sends,
                    recvs,
                    after,
                )
            )

        def finish(total):
            g_out[:, first : first + STEP] = total

        z = line_scatter(
            nt,
            me_t,
            lambda b: gv.at[b, me_d, :, pl.ds(first, STEP)],
            gz.at[c],
            finish,
            sends,
            recvs,
            after,
        )

        def begin():
            at = pl.ds(first, STEP)
            pltpu.make_async_copy(g_ref.at[:, :, :, at], gv.at[:, :, :, at], lsem.at[c]).wait()
            if c == chunks - 1:
                for t in range(nt):
                    for d in range(nd):
                        gv[t, d, :, cols - 128 :] = gv[t, d, :, cols - 128 :] + gg_ref[d]
            for q in cubes:
                q[0]()

        def both(k):
            def run():
                for q in cubes:
                    q[k]()

            return run

        def meet():
            for q in cubes:
                q[bits]()
            z[0]()

        return [begin] + [both(k) for k in range(1, bits)] + [meet] + z[1:]

    def u_finish(total):
        u_out[...] = total

    def e_finish(total):
        e_out[...] = total

    jobs.append((0, a_job))
    jobs.append((0, line_scatter(nt, me_t, lambda b: u_ref.at[b], uz, u_finish, sends, recvs, after)))
    jobs.append((1, line_scatter(nt, me_t, lambda b: e_ref.at[b], ez, e_finish, sends, recvs, after)))
    for c in range(chunks):
        jobs.append((c, chunk_job(c)))
    run_jobs(jobs, after)


def scatter_all(nt, nd, g, a, u, e, gg, tt):
    bits = nd.bit_length() - 1
    rows, cols = g.shape[2:]
    wide = a.shape[2]
    chunks = cols // STEP
    total = (chunks + 2) * 2 * nt + (2 * chunks + 1) * bits
    return pl.pallas_call(
        partial(scatter_kernel, nt, nd),
        out_shape=(
            jax.ShapeDtypeStruct((rows, cols), F32),
            jax.ShapeDtypeStruct((rows, wide), F32),
            jax.ShapeDtypeStruct(u.shape[1:], F32),
            jax.ShapeDtypeStruct(e.shape[1:], F32),
        ),
        in_specs=[ANY] + [VMEM] * 5,
        out_specs=(VMEM,) * 4,
        scratch_shapes=[
            pltpu.VMEM((nt, nd, rows, cols), BF),
            pltpu.VMEM((2,) + u.shape, BF),
            pltpu.VMEM((2,) + e.shape, BF),
            pltpu.VMEM((chunks, 2, nt, rows, STEP), BF),
        ]
        + [pltpu.VMEM((1 << (bits - 1 - k), rows, wide), BF) for k in range(bits)]
        + [pltpu.VMEM((2 * chunks, 1 << (bits - 1 - k), nt, rows, STEP // 2), BF) for k in range(bits)]
        + [
            pltpu.SemaphoreType.DMA((total,)),
            pltpu.SemaphoreType.DMA((total,)),
            pltpu.SemaphoreType.DMA((chunks,)),
        ],
        compiler_params=pltpu.CompilerParams(collective_id=1, has_side_effects=True, vmem_limit_bytes=LIMIT),
        name="scatter_all",
    )(g, a, u, e, gg, tt)


def build_strips(strip, line, heads):
    block = strip.shape[1]
    width = strip.shape[2]
    row = lax.broadcasted_iota(jnp.int32, (8, width), 0)
    for h in range(heads):
        x = jnp.broadcast_to(line[h : h + 1, :], (8, width))
        for b in range(3):
            x = jnp.where((row >> b) % 2 == 1, pltpu.roll(x, 1 << b, 1), x)
        strip[h, 0:8, :] = x
        n = 8
        while n < block:
            strip[h, n : 2 * n, :] = pltpu.roll(strip[h, 0:n, :], n, 1)
            n *= 2


def bias_lines(bl_ref, tab_ref):
    width = bl_ref.shape[1]
    buckets = tab_ref.shape[1]
    hot = bl_ref[...] == lax.broadcasted_iota(jnp.int32, (buckets, width), 0)
    line = dot(tab_ref[...], hot.astype(F32).astype(BF))
    return jnp.where(bl_ref[...] >= 0, line, MASKED), hot


def self_forward_kernel(
    heads, tok_ref, wa_ref, g_ref, segc_ref, segr_ref, bl_ref, tab_ref, qkv_ref, attn_ref, lse_ref, strip, qs, ks, vs, os
):
    nt, block = tok_ref.shape[:2]
    hw = heads * DK
    line, _ = bias_lines(bl_ref, tab_ref)
    build_strips(strip, line, heads)
    for i in range(nt):
        x = tok_ref[i].astype(F32)
        n = (x * norm_scale(x) * g_ref[...]).astype(BF)
        y = dot(n, wa_ref[:, : 3 * hw]).astype(BF)
        qkv_ref[i] = y
        for h in range(heads):
            for which, ref in enumerate((qs, ks, vs)):
                at = which * hw + h * DK
                ref[h, i * block : (i + 1) * block, :] = y[:, at : at + DK]

    def head(h, carry):
        for i in range(nt):
            mine = slice(i * block, (i + 1) * block)
            seen = (i + 1) * block
            s = dot_nt(qs[h, mine, :], ks[h, :seen, :])
            s = s + strip[h, :, (nt - 1 - i) * block : (nt - 1 - i) * block + seen]
            s = jnp.where(segc_ref[mine, :] == segr_ref[:, :seen], s, MASKED)
            top = jnp.max(s, axis=-1, keepdims=True)
            p = jnp.exp(s - top)
            total = jnp.sum(p, axis=-1, keepdims=True)
            o = dot(p.astype(BF), vs[h, :seen, :]) / total
            os[h, mine, :] = o
            lse_ref[h, mine, :] = top + jnp.log(total)
        return carry

    lax.fori_loop(0, heads, head, 0)
    for i in range(nt):
        mine = slice(i * block, (i + 1) * block)
        attn_ref[i] = jnp.concatenate([os[h, mine, :] for h in range(heads)], axis=1).astype(BF)


def self_forward(heads, tok, wa, g, segc, segr, bl, tab):
    nt, block, width = tok.shape
    length = nt * block
    hw = heads * DK
    return pl.pallas_call(
        partial(self_forward_kernel, heads),
        out_shape=(
            jax.ShapeDtypeStruct((nt, block, 3 * hw), BF),
            jax.ShapeDtypeStruct((nt, block, hw), BF),
            jax.ShapeDtypeStruct((heads, length, 1), F32),
        ),
        in_specs=[VMEM] * 7,
        out_specs=(VMEM,) * 3,
        scratch_shapes=[pltpu.VMEM((heads, block, length + block), F32)]
        + [pltpu.VMEM((heads, length, DK), BF)] * 3
        + [pltpu.VMEM((heads, length, DK), F32)],
        compiler_params=pltpu.CompilerParams(vmem_limit_bytes=LIMIT),
        name="self_forward",
    )(tok, wa, g, segc, segr, bl, tab)


def self_backward_kernel(
    heads,
    tok_ref,
    wa_ref,
    g_ref,
    segc_ref,
    segr_ref,
    bl_ref,
    tab_ref,
    qkv_ref,
    attn_ref,
    lse_ref,
    dattn_ref,
    u_ref,
    ga_ref,
    gain_ref,
    table_ref,
    strip,
    dstrip,
    qs,
    ks,
    vs,
    das,
    delta,
    dq,
    dkt,
    dvt,
    norms,
    dqkv,
):
    nt, block = tok_ref.shape[:2]
    hw = heads * DK
    length = nt * block
    line, hot = bias_lines(bl_ref, tab_ref)
    build_strips(strip, line, heads)
    for i in range(nt):
        mine = slice(i * block, (i + 1) * block)
        y = qkv_ref[i]
        da = dattn_ref[i]
        prod = da.astype(F32) * attn_ref[i].astype(F32)
        for h in range(heads):
            part = slice(h * DK, (h + 1) * DK)
            for which, ref in enumerate((qs, ks, vs)):
                at = which * hw + h * DK
                ref[h, mine, :] = y[:, at : at + DK]
            das[h, mine, :] = da[:, part]
            delta[h, mine, :] = jnp.sum(prod[:, part], axis=1, keepdims=True)
    dstrip[...] = jnp.zeros_like(dstrip)
    dkt[...] = jnp.zeros_like(dkt)
    dvt[...] = jnp.zeros_like(dvt)

    def head(h, carry):
        for i in range(nt):
            mine = slice(i * block, (i + 1) * block)
            seen = (i + 1) * block
            off = (nt - 1 - i) * block
            q = qs[h, mine, :]
            da = das[h, mine, :]
            s = dot_nt(q, ks[h, :seen, :])
            s = s + strip[h, :, off : off + seen]
            s = jnp.where(segc_ref[mine, :] == segr_ref[:, :seen], s, MASKED)
            p = jnp.exp(s - lse_ref[h, mine, :])
            dp = dot_nt(da, vs[h, :seen, :])
            ds = p * (dp - delta[h, mine, :])
            low = ds.astype(BF)
            dq[h, mine, :] = dot(low, ks[h, :seen, :])
            dkt[h, :, :seen] += dot_tn(q, low)
            dvt[h, :, :seen] += dot_tn(da, p.astype(BF))
            dstrip[h, :, off : off + seen] += ds
        return carry

    lax.fori_loop(0, heads, head, 0)
    lines = []
    for h in range(heads):
        n = block // 2
        while n >= 8:
            dstrip[h, 0:n, :] = dstrip[h, 0:n, :] + pltpu.roll(dstrip[h, n : 2 * n, :], length + block - n, 1)
            n //= 2
        x = dstrip[h, 0:8, :]
        row = lax.broadcasted_iota(jnp.int32, x.shape, 0)
        for b in range(3):
            x = jnp.where((row >> b) % 2 == 1, pltpu.roll(x, length + block - (1 << b), 1), x)
        lines.append(jnp.sum(x, axis=0, keepdims=True))
    lines = jnp.concatenate(lines + [jnp.zeros((8 - heads, length + block), F32)], axis=0)
    table = lax.dot_general(
        lines,
        hot.astype(F32),
        (((1,), (1,)), ((), ())),
        precision=lax.Precision.HIGHEST,
        preferred_element_type=F32,
    )
    table_ref[...] = jnp.concatenate([table, jnp.zeros((8, 128 - table.shape[1]), F32)], axis=1)
    gain = jnp.zeros(gain_ref.shape, F32)
    for i in range(nt):
        mine = slice(i * block, (i + 1) * block)
        pieces = [dq[h, mine, :] for h in range(heads)]
        pieces += [dkt[h, :, mine].T for h in range(heads)]
        pieces += [dvt[h, :, mine].T for h in range(heads)]
        low = jnp.concatenate(pieces, axis=1).astype(BF)
        dqkv[mine, :] = low
        x = tok_ref[i].astype(F32)
        hat = x * norm_scale(x)
        norms[mine, :] = (hat * g_ref[...]).astype(BF)
        u = dot_nt(low, wa_ref[:, : 3 * hw])
        gain = gain + jnp.sum(u * hat, axis=0, keepdims=True)
        u_ref[i] = u.astype(BF)
    gain_ref[...] = gain
    ga_ref[:, : 3 * hw] = dot_tn(norms[...], dqkv[...]).astype(BF)
    ga_ref[:, 3 * hw :] = jnp.zeros((ga_ref.shape[0], ga_ref.shape[1] - 3 * hw), BF)


def self_backward(heads, tok, wa, g, segc, segr, bl, tab, qkv, attn, lse, dattn):
    nt, block, width = tok.shape
    length = nt * block
    hw = heads * DK
    return pl.pallas_call(
        partial(self_backward_kernel, heads),
        out_shape=(
            jax.ShapeDtypeStruct((nt, block, width), BF),
            jax.ShapeDtypeStruct(wa.shape, BF),
            jax.ShapeDtypeStruct((1, width), F32),
            jax.ShapeDtypeStruct((8, 128), F32),
        ),
        in_specs=[VMEM] * 11,
        out_specs=(VMEM,) * 4,
        scratch_shapes=[pltpu.VMEM((heads, block, length + block), F32)] * 2
        + [pltpu.VMEM((heads, length, DK), BF)] * 4
        + [pltpu.VMEM((heads, length, 1), F32), pltpu.VMEM((heads, length, DK), F32)]
        + [pltpu.VMEM((heads, DK, length), F32)] * 2
        + [pltpu.VMEM((length, width), BF), pltpu.VMEM((length, 3 * hw), BF)],
        compiler_params=pltpu.CompilerParams(vmem_limit_bytes=LIMIT),
        name="self_backward",
    )(tok, wa, g, segc, segr, bl, tab, qkv, attn, lse, dattn)


def middle_kernel(
    heads,
    ff,
    tok_ref,
    enc_ref,
    attn_ref,
    og_ref,
    gains_ref,
    w_hbm,
    layer_ref,
    one_ref,
    denc_ref,
    gain_ref,
    dattn_ref,
    g_hbm,
    w,
    g,
    h1_ref,
    h2_ref,
    n1_ref,
    n2_ref,
    acc_ref,
    dn_ref,
    g2_ref,
    denc,
    qc,
    kv,
    ac,
    oc,
    lse,
    dkv,
    insem,
    outsem,
):
    nt = w.shape[0]
    hw = heads * DK
    cols = w.shape[2]
    f0, f1, f2 = 0, ff, 2 * ff
    kv0 = 3 * ff
    q0 = kv0 + 2 * hw
    c0 = q0 + hw
    s0 = c0 + hw
    end = s0 + hw
    ffn = pl.ds(0, 3 * ff)
    att = pl.ds(3 * ff, cols - 3 * ff)
    loads = [pltpu.make_async_copy(w_hbm.at[t, :, att], w.at[t, :, att], insem.at[0, t]) for t in range(nt)]
    loads += [pltpu.make_async_copy(w_hbm.at[t, :, ffn], w.at[t, :, ffn], insem.at[1, t]) for t in range(nt)]
    for copy in loads:
        copy.start()

    def load_wait(which, t):
        at = att if which == 0 else ffn
        pltpu.make_async_copy(w_hbm.at[t, :, at], w.at[t, :, at], insem.at[which, t]).wait()

    def store(which, t):
        at = att if which == 0 else ffn
        return pltpu.make_async_copy(g.at[t, :, at], g_hbm.at[t, :, at], outsem.at[which, t])

    acc_ref[...] = tok_ref[...].astype(F32)

    def self_out(t, carry):
        load_wait(0, t)
        acc_ref[...] += dot_nt(attn_ref[t], w[t, :, s0:end])
        return carry

    lax.fori_loop(0, nt, self_out, 0)
    h1 = acc_ref[...]
    h1_ref[...] = h1
    n1_ref[...] = (h1 * norm_scale(h1) * gains_ref[1:2, :]).astype(BF)

    def cross(t, carry):
        q = dot(n1_ref[...], w[t, :, q0:c0]).astype(BF)
        both = dot(enc_ref[...], w[t, :, kv0:q0]).astype(BF)
        qc[t] = q
        kv[t] = both
        outs = []
        for h in range(heads):
            part = slice(h * DK, (h + 1) * DK)
            s = dot_nt(q[:, part], both[:, part])
            top = jnp.max(s, axis=-1, keepdims=True)
            p = jnp.exp(s - top)
            total = jnp.sum(p, axis=-1, keepdims=True)
            lse[t, h] = top + jnp.log(total)
            outs.append(dot(p.astype(BF), both[:, hw + h * DK : hw + (h + 1) * DK]) / total)
        a = jnp.concatenate(outs, axis=1).astype(BF)
        ac[t] = a
        acc_ref[...] += dot_nt(a, w[t, :, c0:s0])
        return carry

    lax.fori_loop(0, nt, cross, 0)
    h2 = acc_ref[...]
    h2_ref[...] = h2
    n2_ref[...] = (h2 * norm_scale(h2) * gains_ref[2:3, :]).astype(BF)
    dn_ref[...] = jnp.zeros_like(dn_ref)

    def units(t, carry):
        load_wait(1, t)
        n2 = n2_ref[...]
        og = og_ref[...]
        gate = dot(n2, w[t, :, f0:f1])
        up = dot(n2, w[t, :, f1:f2])
        dinner = dot(og, w[t, :, f2 : 3 * ff])
        sq = gate * gate
        th = jnp.tanh(0.7978845608028654 * (gate + 0.044715 * (gate * sq)))
        cdf = 0.5 * (1.0 + th)
        act = gate * cdf
        slope = cdf + gate * (0.5 * (1.0 - th * th)) * (0.7978845608028654 * (1.0 + 0.134145 * sq))
        inner = (act * up).astype(BF)
        dgate = (dinner * up * slope).astype(BF)
        dup = (dinner * act).astype(BF)
        acc_ref[...] += dot_nt(inner, w[t, :, f2 : 3 * ff])
        dn_ref[...] += dot_nt(dgate, w[t, :, f0:f1]) + dot_nt(dup, w[t, :, f1:f2])
        g[t, :, f0:f1] = dot_tn(n2, dgate).astype(BF)
        g[t, :, f1:f2] = dot_tn(n2, dup).astype(BF)
        g[t, :, f2 : 3 * ff] = dot_tn(og, inner).astype(BF)
        store(1, t).start()
        return carry

    lax.fori_loop(0, nt, units, 0)
    layer_ref[...] = acc_ref[...].astype(BF)
    h2 = h2_ref[...]
    back, gain2 = norm_back(h2, norm_scale(h2), gains_ref[2:3, :], dn_ref[...])
    g2 = og_ref[...].astype(F32) + back
    acc_ref[...] = g2
    g2_ref[...] = g2.astype(BF)
    dn_ref[...] = jnp.zeros_like(dn_ref)
    denc[...] = jnp.zeros_like(denc)

    def cross_back(t, carry):
        g2 = g2_ref[...]
        a = ac[t]
        da = dot(g2, w[t, :, c0:s0]).astype(BF)
        g[t, :, c0:s0] = dot_tn(g2, a).astype(BF)
        prod = da.astype(F32) * a.astype(F32)
        q = qc[t]
        both = kv[t]
        dqs = []
        for h in range(heads):
            part = slice(h * DK, (h + 1) * DK)
            qh, kh = q[:, part], both[:, part]
            vh, dah = both[:, hw + h * DK : hw + (h + 1) * DK], da[:, part]
            p = jnp.exp(dot_nt(qh, kh) - lse[t, h])
            delta = jnp.sum(prod[:, part], axis=1, keepdims=True)
            ds = (p * (dot_nt(dah, vh) - delta)).astype(BF)
            dqs.append(dot(ds, kh))
            dkv[h * DK : (h + 1) * DK, :] = dot_tn(qh, ds)
            dkv[hw + h * DK : hw + (h + 1) * DK, :] = dot_tn(dah, p.astype(BF))
        dq = jnp.concatenate(dqs, axis=1).astype(BF)
        dboth = dkv[...].astype(BF)
        g[t, :, q0:c0] = dot_tn(n1_ref[...], dq).astype(BF)
        g[t, :, kv0:q0] = lax.dot_general(
            enc_ref[...], dboth, (((0,), (1,)), ((), ())), preferred_element_type=F32
        ).astype(BF)
        dn_ref[...] += dot_nt(dq, w[t, :, q0:c0])
        denc[...] += lax.dot_general(
            dboth, w[t, :, kv0:q0], (((0,), (1,)), ((), ())), preferred_element_type=F32
        )
        return carry

    lax.fori_loop(0, nt, cross_back, 0)
    denc_ref[...] = denc[...].astype(BF)
    h1 = h1_ref[...]
    back, gain1 = norm_back(h1, norm_scale(h1), gains_ref[1:2, :], dn_ref[...])
    g1 = acc_ref[...] + back
    one_ref[...] = g1
    g2_ref[...] = g1.astype(BF)
    gain_ref[...] = jnp.concatenate([gain1, gain2, jnp.zeros((6, gain1.shape[1]), F32)], axis=0)

    def self_out_back(t, carry):
        low = g2_ref[...]
        dattn_ref[t] = dot(low, w[t, :, s0:end]).astype(BF)
        tail = dot_tn(low, attn_ref[t])
        g[t, :, s0:cols] = jnp.concatenate([tail, jnp.zeros((tail.shape[0], cols - end), F32)], axis=1).astype(BF)
        store(0, t).start()
        return carry

    lax.fori_loop(0, nt, self_out_back, 0)
    for t in range(nt):
        store(1, t).wait()
        store(0, t).wait()


def middle(heads, ff, tok, enc, attn, og, gains, w):
    nt, _, cols = w.shape
    rows, width = tok.shape
    states = enc.shape[0]
    hw = heads * DK
    return pl.pallas_call(
        partial(middle_kernel, heads, ff),
        out_shape=(
            jax.ShapeDtypeStruct((rows, width), BF),
            jax.ShapeDtypeStruct((rows, width), F32),
            jax.ShapeDtypeStruct((states, width), BF),
            jax.ShapeDtypeStruct((8, width), F32),
            jax.ShapeDtypeStruct((nt, rows, hw), BF),
            jax.ShapeDtypeStruct(w.shape, BF),
        ),
        in_specs=[VMEM] * 5 + [ANY],
        out_specs=(VMEM,) * 5 + (ANY,),
        scratch_shapes=[
            pltpu.VMEM(w.shape, BF),
            pltpu.VMEM(w.shape, BF),
            pltpu.VMEM((rows, width), F32),
            pltpu.VMEM((rows, width), F32),
            pltpu.VMEM((rows, width), BF),
            pltpu.VMEM((rows, width), BF),
            pltpu.VMEM((rows, width), F32),
            pltpu.VMEM((rows, width), F32),
            pltpu.VMEM((rows, width), BF),
            pltpu.VMEM((states, width), F32),
            pltpu.VMEM((nt, rows, hw), BF),
            pltpu.VMEM((nt, states, 2 * hw), BF),
            pltpu.VMEM((nt, rows, hw), BF),
            pltpu.VMEM((8, 128), F32),
            pltpu.VMEM((nt, heads, rows, 1), F32),
            pltpu.VMEM((2 * hw, states), F32),
            pltpu.SemaphoreType.DMA((2, nt)),
            pltpu.SemaphoreType.DMA((2, nt)),
        ],
        compiler_params=pltpu.CompilerParams(vmem_limit_bytes=LIMIT),
        name="middle",
    )(tok, enc, attn, og, gains, w)


def per_device(
    tokens,
    encoder,
    segments,
    rel_bucket,
    out_grad,
    self_q,
    self_k,
    self_v,
    self_o,
    cross_q,
    cross_k,
    cross_v,
    cross_o,
    ffn_gate,
    ffn_up,
    ffn_down,
    bias_table,
    norm_gains,
):
    nt, nd = lax.axis_size("tensor"), lax.axis_size("dp")
    part, hw = self_q.shape
    ff = ffn_gate.shape[1]
    heads = hw // DK
    rows, width = tokens.shape
    length = rows * nt
    buckets = bias_table.shape[0]
    wa = jnp.concatenate([self_q, self_k, self_v, jnp.pad(norm_gains.T, ((0, 0), (0, 128 - norm_gains.shape[0])))], axis=1)
    wb = jnp.concatenate([ffn_gate, ffn_up, ffn_down.T, cross_k, cross_v, cross_q, cross_o.T, self_o.T], axis=1)
    used = wb.shape[1]
    cols = -(-(used + 3) // STEP) * STEP
    wb = jnp.pad(wb, ((0, 0), (0, cols - used)))
    tok_all, enc_all, wa_all, wb_all = gather_all(nt, nd, tokens, encoder, wa, wb)
    wa_full = wa_all.reshape(nd * part, wa.shape[1])
    wb_full = wb_all.reshape(nt, nd * part, cols)
    gains = jnp.pad(wa_full[:, 3 * hw : 3 * hw + 3].T.astype(F32), ((0, 5), (0, 0)))
    top = (nt - 1) * rows
    blank = jnp.full((length - 1 - top,), -1, jnp.int32)
    bl = jnp.concatenate(
        [rel_bucket[: top + 1][::-1], blank, jnp.full((1,), -1, jnp.int32), rel_bucket[top + 1 : length][::-1]]
    )[None, :]
    tab = jnp.pad(bias_table.T, ((0, 8 - heads), (0, 0)))
    segr = segments
    segc = segments.T
    g0 = gains[0:1]
    qkv, attn, lse = self_forward(heads, tok_all, wa_full, g0, segc, segr, bl, tab)
    mine = exchange(nt, attn, 2)
    layer_out, grad_one, denc, gain12, dmine, gb = middle(
        heads, ff, tokens, enc_all.reshape(nt * encoder.shape[0], width), mine, out_grad, gains, wb_full
    )
    dattn = exchange(nt, dmine, 3)
    u, ga, gain0, table = self_backward(
        heads, tok_all, wa_full, g0, segc, segr, bl, tab, qkv, attn, lse, dattn
    )
    gg = jnp.concatenate([gain0, gain12[0:2]], axis=0).T.astype(BF)
    lane = used - (cols - 128)
    gg = jnp.pad(gg, ((0, 0), (lane, 128 - lane - 3))).reshape(nd, part, 128)
    gsum, asum, usum, esum = scatter_all(
        nt,
        nd,
        gb.reshape(nt, nd, part, cols),
        ga.reshape(nd, part, wa.shape[1]),
        u,
        denc.reshape((nt,) + encoder.shape),
        gg,
        table,
    )
    x = tokens.astype(F32)
    back, _ = norm_back(x, norm_scale(x), g0, usum)
    tokens_grad = grad_one + back
    at = 3 * ff
    ck, cv, cq, co, so = (gsum[:, at + n * hw : at + (n + 1) * hw] for n in range(5))
    return (
        layer_out,
        tokens_grad,
        esum,
        asum[:, :hw],
        asum[:, hw : 2 * hw],
        asum[:, 2 * hw : 3 * hw],
        so.T,
        cq,
        ck,
        cv,
        co.T,
        gsum[:, :ff],
        gsum[:, ff : 2 * ff],
        gsum[:, 2 * ff : 3 * ff].T,
        asum[:heads, 3 * hw : 3 * hw + buckets].T,
        gsum[:, used : used + 3].T,
    )


def solution(mesh):
    rows = P(("dp", "tensor"), None)
    left = P("dp", "tensor")
    right = P("tensor", "dp")
    return jax.shard_map(
        per_device,
        mesh=mesh,
        in_specs=(rows, rows, P("dp", None), P(), rows, left, left, left, right, left, left, left, right, left, left, right)
        + (P(None, "tensor"), P(None, "dp")),
        out_specs=(rows, rows, rows, left, left, left, right, left, left, left, right, left, left, right)
        + (P(None, "tensor"), P(None, "dp")),
        check_vma=False,
    )
```

time: 1250 us -> 376 us (0.30); the launches traced: 1230 us -> 375 us
  local copies, waits for them, and re-layouts: 454 us -> 18.5 us
  waiting for transfers between devices: 414 us -> 0 us
  Pallas kernels: 0 us -> 350 us
  blocking collectives: 178 us -> 0 us
  matrix products: 119 us -> 0 us
  other arithmetic: 47.5 us -> 5.82 us
  between operations: 15.9 us -> 0.79 us
    pallas_call x0 -> x7, Pallas kernels: none -> 350 us  [the longest x1 130 us: scatter_all(): pl.pallas_call(partial(scatter_kernel, nt, nd), out_shape=(jax.ShapeDtype...]
    reduce_scatter x14 -> x0, waiting for transfers between devices: 288 us -> none  [the longest x6 169 us: scatter_rows(): lax.psum_scatter(term(jnp.int32(0), lax.axis_size('tensor') * count).asty...]
    rev x4 -> x0, local copies, waits for them, and re-layouts: 185 us -> none  [the longest x2 102 us: skewed_grid(): return grid[:, :, ::-1]]
    all_gather x13 -> x0, blocking collectives: 139 us -> none  [the longest x1 17.8 us: per_device(): encoder_all = lax.all_gather(encoder, 'tensor', axis=0, tiled=True)]
    dot_general x57 -> x0, matrix products: 116 us -> none  [the longest x12 26.4 us: product_nt(): lax.dot_general(left, right, (((1,), (1,)), ((), ())), preferred_element_...]
    unnamed x221 -> x27, local copies, waits for them, and re-layouts: 118 us -> 6.93 us
    reshape x6 -> x0, local copies, waits for them, and re-layouts: 90.9 us -> none  [the longest x2 33.4 us: skewed_grid(): grid = tiled.reshape(heads, block, width + 1)[:, :, :length]]
    all_gather x6 -> x0, waiting for transfers between devices: 86.4 us -> none  [gather_rows(): return lax.all_gather(value, 'tensor', axis=0, tiled=True)]
  transfers between devices with their start and end apart: 24 -> 0, of which waited for: 13 -> 0; matrix products, arithmetic and copies ran while one was open for 45% -> 0% of each run, Pallas kernels for 0% -> 0%
where the time goes in v1:
time: 376 us; the launch traced here: 375 us
  Pallas kernels  350 us (93%)
  local copies, waits for them, and re-layouts  18.5 us (5%)
  other arithmetic  5.82 us (2%)
    pallas_call x1, Pallas kernels, scatter_all(): pl.pallas_call(partial(scatter_kernel, nt, nd), out_shape=(jax.ShapeDtype...  130 us
    pallas_call x1, Pallas kernels, gather_all(): pl.pallas_call(partial(gather_kernel, nt, nd), out_shape=(jax.ShapeDtypeS...  120 us
    pallas_call x1, Pallas kernels, middle(): pl.pallas_call(partial(middle_kernel, heads, ff), out_shape=(jax.ShapeDty...  39.2 us
    pallas_call x2, Pallas kernels, exchange(): pl.pallas_call(partial(exchange_kernel, nt), out_shape=jax.ShapeDtypeStru...  32 us
    pallas_call x1, Pallas kernels, self_backward(): pl.pallas_call(partial(self_backward_kernel, heads), out_shape=(jax.Shape...  17.1 us
    pallas_call x1, Pallas kernels, self_forward(): pl.pallas_call(partial(self_forward_kernel, heads), out_shape=(jax.ShapeD...  11.7 us

profile of v1, /device:TPU:0, one launch (start us, length us, event | category | flops | bytes accessed | tf_op | source)
XLA Modules:
  0.0 375.4 jit_solution(14665310252857709862)
XLA Ops:
  0.6 0.0 copy-start.6
  0.7 0.8 slice.59
  1.4 0.1 reverse.1
  1.5 0.1 slice.86
  1.6 1.3 pad.22.tab_ref
  2.9 0.8 reverse
  3.6 0.1 slice.85
  3.7 0.1 concatenate.15
  3.8 0.6 broadcast_in_dim.9.bl_ref
  4.4 0.8 copy.44
  5.2 0.9 copy.46
  6.1 0.9 copy.45
  7.0 1.6 fusion.5.wa_ref
  8.6 1.1 concatenate.14
  9.7 0.8 pad.21.wb_ref
  10.5 0.0 copy-done.6
  10.5 1.0 copy.48.segc_ref
  11.6 120.3 %gather_all.1 = (bf16[4,256,768]{2,1,0:T(8,128)(2,1)}, bf16[4,128,768]{2,1,0:T(8,128)(2,1)}, bf16[8,96,704]{2,1,0:T(8,128)(2,1)}, bf16[4,8,96,2560]{3,2,1,0:T(8,128)(2,1)}) custom-call(bf16[256,768]{1,0:T(8,128)(2,1)} %tok_ref.3, bf16[128,768]{1,0:T(8,128)(2,1)} %enc_ref.1, bf16[96,704]{1,0:T(8,128)(2,1)} %fusion.5.wa_ref, bf16[96,2560]{1,0:T(8,128)(2,1)} %pad.21.wb_ref), custom_call_target="tpu_custom_call" | custom-call | tf_op jit(solution)/shard_map/gather_all/pallas_call | solution.py:270
  131.9 1.0 slice_convert_fusion
  132.9 0.1 copy.56
  133.1 0.6 slice_reduce_fusion
  133.7 0.6 pad.23.gains_ref
  134.3 11.7 %self_forward.1 = (bf16[4,256,576]{2,1,0:T(8,128)(2,1)}, bf16[4,256,192]{2,1,0:T(8,128)(2,1)}, f32[3,1024,1]{2,1,0:T(8,128)}) custom-call(bf16[4,256,768]{2,1,0:T(8,128)(2,1)} %get-tuple-element.38.tok_ref, bf16[768,704]{1,0:T(8,128)(2,1)} %bitcast.32, f32[1,768]{1,0:T(1,128)} %get-tuple-element.104.g_ref, s32[1024,1]{1,0:T(8,128)} %copy.48.segc_ref, ...), custom_call_target="tpu_custom_call" | custom-call | tf_op jit(solution)/shard_map/self_forward/pallas_call | solution.py:639
  146.0 15.8 %exchange.2.attn_ref = bf16[4,256,192]{2,1,0:T(8,128)(2,1)} custom-call(bf16[4,256,192]{2,1,0:T(8,128)(2,1)} %get-tuple-element.40.x_ref.attn_ref), custom_call_target="tpu_custom_call" | custom-call | tf_op jit(solution)/shard_map/exchange/pallas_call | solution.py:312
  161.8 39.2 %middle.1 = (bf16[256,768]{1,0:T(8,128)(2,1)}, f32[256,768]{1,0:T(8,128)}, bf16[512,768]{1,0:T(8,128)(2,1)}, f32[8,768]{1,0:T(8,128)}, bf16[4,256,192]{2,1,0:T(8,128)(2,1)}, /*index=5*/bf16[4,768,2560]{2,1,0:T(8,128)(2,1)}) custom-call(bf16[256,768]{1,0:T(8,128)(2,1)} %tok_ref.3, bf16[512,768]{1,0:T(8,128)(2,1)} %bitcast.36, ...), custom_call_target="tpu_custom_call" | custom-call | tf_op jit(solution)/shard_map/middle/pallas_call | solution.py:978
  201.0 0.7 slice.87
  201.7 16.2 %exchange.3.dattn_ref = bf16[4,256,192]{2,1,0:T(8,128)(2,1)} custom-call(bf16[4,256,192]{2,1,0:T(8,128)(2,1)} %get-tuple-element.47.x_ref), custom_call_target="tpu_custom_call" | custom-call | tf_op jit(solution)/shard_map/exchange/pallas_call | solution.py:312
  218.0 17.1 %self_backward.1 = (bf16[4,256,768]{2,1,0:T(8,128)(2,1)}, bf16[768,704]{1,0:T(8,128)(2,1)}, f32[1,768]{1,0:T(1,128)}, f32[8,128]{1,0:T(8,128)}) custom-call(bf16[4,256,768]{2,1,0:T(8,128)(2,1)} %get-tuple-element.38.tok_ref, bf16[768,704]{1,0:T(8,128)(2,1)} %bitcast.33, f32[1,768]{1,0:T(1,128)} %get-tuple-element.104.g_ref, s32[1024,1]{1,0:T(8,128)} %copy.48.segc_ref, ...), custom_call_target="tpu_custom_call" | custom-call | tf_op jit(solution)/shard_map/self_backward/pallas_call | solution.py:771
  235.0 0.7 convert.8
  235.7 0.2 copy.55
  235.9 0.8 pad.24.clone
  236.7 0.0 copy-start
  236.7 0.0 copy-start.3
  236.7 130.0 %scatter_all.1 = (f32[96,2560]{1,0:T(8,128)}, f32[96,704]{1,0:T(8,128)}, f32[256,768]{1,0:T(8,128)}, f32[128,768]{1,0:T(8,128)}) custom-call(bf16[4,8,96,2560]{3,2,1,0:T(8,128)(2,1)} %bitcast.30, bf16[8,96,704]{2,1,0:T(8,128)(2,1)} %bitcast.34, bf16[4,256,768]{2,1,0:T(8,128)(2,1)} %get-tuple-element.49.u_ref, bf16[4,128,768]{2,1,0:T(8,128)(2,1)} %bitcast.37, ...), custom_call_target="tpu_custom_call" | custom-call | tf_op jit(solution)/shard_map/scatter_all/pallas_call | solution.py:546
  366.7 0.0 copy-start.1
  366.7 1.4 slice_bitcast_fusion.4
  368.1 0.0 copy-done
  368.1 1.4 fusion
  369.5 0.0 copy-start.2
  369.5 0.0 copy-start.5
  369.5 0.0 copy-done.3
  369.5 0.0 copy-done.1
  369.5 1.1 fusion.3
  370.6 0.1 copy-done.2
  370.7 0.1 slice_bitcast_fusion.3
  370.8 0.7 copy.53
  371.5 0.0 copy-done.5
  371.5 0.0 copy-start.4
  371.5 0.9 slice_bitcast_fusion.1
  372.4 0.8 slice_bitcast_fusion
  373.2 0.7 copy.52
  373.9 0.7 copy.51
  374.7 0.0 copy-done.4
  374.7 0.7 copy.58
  (3 shorter events, 0.0 us)
Async XLA Ops:
  0.6 9.9 %copy-start.6 = (s32[1,1024]{1,0:T(1,128)S(1)}, s32[1,1024]{1,0:T(1,128)}, u32[]{:S(2)}) copy-start(s32[1,1024]{1,0:T(1,128)} %segr_ref.3) | copy-start | bytes 12292
  236.7 131.4 %copy-start = (bf16[256,768]{1,0:T(8,128)(2,1)S(1)}, bf16[256,768]{1,0:T(8,128)(2,1)}, u32[]{:S(2)}) copy-start(bf16[256,768]{1,0:T(8,128)(2,1)} %tok_ref.3) | copy-start | bytes 1179652
  236.7 132.8 %copy-start.3 = (f32[256,768]{1,0:T(8,128)S(1)}, f32[256,768]{1,0:T(8,128)}, u32[]{:S(2)}) copy-start(f32[256,768]{1,0:T(8,128)} %get-tuple-element.43) | copy-start | bytes 2359300
  366.7 2.8 copy-start.1
  369.5 1.3 copy-start.2
  369.5 2.0 copy-start.5
  371.5 3.2 copy-start.4

commit v2 on v1

--- a/solution.py
+++ b/solution.py
@@ -17,6 +17,11 @@
 ANY = pl.BlockSpec(memory_space=pl.ANY)
 LIMIT = 62 * 1024 * 1024
 STEP = 256
+SPACE = 2
+PIECE = 32
+TOK0 = 2
+TOKR = 1
+ROWR = 1
 
 
 def dot(a, b):
@@ -102,11 +107,12 @@
 
 
 def run_jobs(jobs, after):
-    last = max(start + len(stages) for start, stages in jobs)
-    for tick in range(last):
-        for start, stages in jobs:
-            if 0 <= tick - start < len(stages):
-                stages[tick - start]()
+    events = []
+    for number, (start, stages, ticks) in enumerate(jobs):
+        for tick, stage in zip(ticks, stages, strict=True):
+            events.append((start + tick, start, number, stage))
+    for event in sorted(events, key=lambda e: e[:3]):
+        event[3]()
     for fn in after:
         fn()
 
@@ -205,7 +211,11 @@
     half = STEP // 2
     jobs = []
     jobs.append(
-        (0, cube_gather(nd, me_d, orders[0], wa_ref, lambda d: wa_out.at[d], lambda n: wa_out.at[pl.ds(0, n)], sends, recvs, after))
+        (
+            0,
+            cube_gather(nd, me_d, orders[0], wa_ref, lambda d: wa_out.at[d], lambda n: wa_out.at[pl.ds(0, n)], sends, recvs, after),
+            [SPACE * k for k in range(bits + 1)],
+        )
     )
 
     def chunk_job(c):
@@ -250,12 +260,19 @@
 
         return z[:-1] + [meet] + [both(k) for k in range(1, bits + 1)]
 
-    tok_job = line_gather(nt, me_t, tok_ref, lambda t: tok_out.at[t], sends, recvs, after)
-    enc_job = line_gather(nt, me_t, enc_ref, lambda t: enc_out.at[t], sends, recvs, after)
+
+    def row_job(ref, out, n):
+        at = pl.ds(n * PIECE, PIECE)
+        return line_gather(nt, me_t, ref.at[at], lambda t: out.at[t, at], sends, recvs, after)
+
+    ticks = list(range(nt)) + [nt - 1 + SPACE * k for k in range(1, bits + 1)]
     for c in range(chunks):
-        jobs.append((c, chunk_job(c)))
-    jobs.append((2, tok_job))
-    jobs.append((5, enc_job))
+        jobs.append((c, chunk_job(c), ticks))
+    number = TOK0
+    for ref, out in ((tok_ref, tok_out), (enc_ref, enc_out)):
+        for n in range(ref.shape[0] // PIECE):
+            jobs.append((number // TOKR, row_job(ref, out, n), list(range(nt))))
+            number += 1
     pltpu.make_async_copy(wb_ref, wb_out.at[me_t, me_d], lsem.at[3]).wait()
     for n in range(3):
         src, dst = locals_[n]
@@ -266,7 +283,8 @@
 def gather_all(nt, nd, tok, enc, wa, wb):
     bits = nd.bit_length() - 1
     chunks = wb.shape[1] // STEP
-    total = (chunks + 2) * 2 * (nt - 1) + (2 * chunks + 1) * bits
+    lines = chunks + (tok.shape[0] + enc.shape[0]) // PIECE
+    total = lines * 2 * (nt - 1) + (2 * chunks + 1) * bits
     return pl.pallas_call(
         partial(gather_kernel, nt, nd),
         out_shape=(
@@ -408,9 +426,9 @@
                     wait_bytes(recv.at[1, here], sem[1, here][1])
                 total = value(here)[...].astype(F32)
                 if here > 0:
-                    total = total + recv[0, here].astype(F32)
+                    total = total + recv.at[0, here][...].astype(F32)
                 if here < nt - 1:
-                    total = total + recv[1, here].astype(F32)
+                    total = total + recv.at[1, here][...].astype(F32)
                 finish(total)
 
     def done():
@@ -523,17 +541,23 @@
 
         return [begin] + [both(k) for k in range(1, bits)] + [meet] + z[1:]
 
-    def u_finish(total):
-        u_out[...] = total
-
-    def e_finish(total):
-        e_out[...] = total
-
-    jobs.append((0, a_job))
-    jobs.append((0, line_scatter(nt, me_t, lambda b: u_ref.at[b], uz, u_finish, sends, recvs, after)))
-    jobs.append((1, line_scatter(nt, me_t, lambda b: e_ref.at[b], ez, e_finish, sends, recvs, after)))
+    def row_job(ref, recv, out, n):
+        at = pl.ds(n * PIECE, PIECE)
+
+        def finish(total):
+            out[at, :] = total
+
+        return line_scatter(nt, me_t, lambda b: ref.at[b, at], recv.at[:, :, at], finish, sends, recvs, after)
+
+    ticks = [SPACE * k for k in range(bits)] + [SPACE * bits + k for k in range(nt)]
+    jobs.append((0, a_job, [SPACE * k for k in range(bits + 1)] + [SPACE * bits]))
     for c in range(chunks):
-        jobs.append((c, chunk_job(c)))
+        jobs.append((c, chunk_job(c), ticks))
+    number = 0
+    for ref, recv, out in ((u_ref, uz, u_out), (e_ref, ez, e_out)):
+        for n in range(out.shape[0] // PIECE):
+            jobs.append((number // ROWR, row_job(ref, recv, out, n), list(range(nt))))
+            number += 1
     run_jobs(jobs, after)
 
 
@@ -542,7 +566,8 @@
     rows, cols = g.shape[2:]
     wide = a.shape[2]
     chunks = cols // STEP
-    total = (chunks + 2) * 2 * nt + (2 * chunks + 1) * bits
+    lines = chunks + (u.shape[1] + e.shape[1]) // PIECE
+    total = lines * 2 * nt + (2 * chunks + 1) * bits
     return pl.pallas_call(
         partial(scatter_kernel, nt, nd),
         out_shape=(

time: 376 us -> 321 us (0.85); the launches traced: 375 us -> 315 us
  Pallas kernels: 350 us -> 289 us
    pallas_call x1, Pallas kernels: 130 us -> 98.9 us  [scatter_all(): pl.pallas_call(partial(scatter_kernel, nt, nd), out_shape=(jax.ShapeDtype...]
    pallas_call x1, Pallas kernels: 120 us -> 91.1 us  [gather_all(): pl.pallas_call(partial(gather_kernel, nt, nd), out_shape=(jax.ShapeDtypeS...]
where the time goes in v2:
time: 321 us; the launch traced here: 315 us
  Pallas kernels  289 us (90%)
  local copies, waits for them, and re-layouts  18.5 us (6%)
  other arithmetic  5.82 us (2%)
    pallas_call x1, Pallas kernels, scatter_all(): pl.pallas_call(partial(scatter_kernel, nt, nd), out_shape=(jax.ShapeDtype...  98.9 us
    pallas_call x1, Pallas kernels, gather_all(): pl.pallas_call(partial(gather_kernel, nt, nd), out_shape=(jax.ShapeDtypeS...  91.1 us
    pallas_call x1, Pallas kernels, middle(): pl.pallas_call(partial(middle_kernel, heads, ff), out_shape=(jax.ShapeDty...  39.2 us
    pallas_call x2, Pallas kernels, exchange(): pl.pallas_call(partial(exchange_kernel, nt), out_shape=jax.ShapeDtypeStru...  31.5 us
    pallas_call x1, Pallas kernels, self_backward(): pl.pallas_call(partial(self_backward_kernel, heads), out_shape=(jax.Shape...  17.1 us
    pallas_call x1, Pallas kernels, self_forward(): pl.pallas_call(partial(self_forward_kernel, heads), out_shape=(jax.ShapeD...  11.7 us
    unnamed x27, local copies, waits for them, and re-layouts  6.93 us

profile of v2, /device:TPU:0, one launch (start us, length us, event | category | flops | bytes accessed | tf_op | source)
XLA Modules:
  0.0 315.0 jit_solution(154497509377590673)
XLA Ops:
  0.6 0.0 copy-start.6
  0.7 0.8 slice.59
  1.4 0.1 reverse.1
  1.5 0.1 slice.86
  1.6 1.3 pad.22.tab_ref
  2.9 0.8 reverse
  3.6 0.1 slice.85
  3.7 0.1 concatenate.15
  3.8 0.6 broadcast_in_dim.9.bl_ref
  4.4 0.8 copy.44
  5.2 0.9 copy.46
  6.1 0.9 copy.45
  7.0 1.6 fusion.5.wa_ref
  8.6 1.1 concatenate.14
  9.7 0.8 pad.21.wb_ref
  10.5 0.0 copy-done.6
  10.5 1.0 copy.48.segc_ref
  11.6 91.1 %gather_all.1 = (bf16[4,256,768]{2,1,0:T(8,128)(2,1)}, bf16[4,128,768]{2,1,0:T(8,128)(2,1)}, bf16[8,96,704]{2,1,0:T(8,128)(2,1)}, bf16[4,8,96,2560]{3,2,1,0:T(8,128)(2,1)}) custom-call(bf16[256,768]{1,0:T(8,128)(2,1)} %tok_ref.3, bf16[128,768]{1,0:T(8,128)(2,1)} %enc_ref.1, bf16[96,704]{1,0:T(8,128)(2,1)} %fusion.5.wa_ref, bf16[96,2560]{1,0:T(8,128)(2,1)} %pad.21.wb_ref), custom_call_target="tpu_custom_call" | custom-call | tf_op jit(solution)/shard_map/gather_all/pallas_call | solution.py:288
  102.7 1.0 slice_convert_fusion
  103.8 0.1 copy.56
  103.9 0.6 slice_reduce_fusion
  104.5 0.6 pad.23.gains_ref
  105.1 11.7 %self_forward.1 = (bf16[4,256,576]{2,1,0:T(8,128)(2,1)}, bf16[4,256,192]{2,1,0:T(8,128)(2,1)}, f32[3,1024,1]{2,1,0:T(8,128)}) custom-call(bf16[4,256,768]{2,1,0:T(8,128)(2,1)} %get-tuple-element.38.tok_ref, bf16[768,704]{1,0:T(8,128)(2,1)} %bitcast.32, f32[1,768]{1,0:T(1,128)} %get-tuple-element.104.g_ref, s32[1024,1]{1,0:T(8,128)} %copy.48.segc_ref, ...), custom_call_target="tpu_custom_call" | custom-call | tf_op jit(solution)/shard_map/self_forward/pallas_call | solution.py:664
  116.8 15.0 %exchange.2.attn_ref = bf16[4,256,192]{2,1,0:T(8,128)(2,1)} custom-call(bf16[4,256,192]{2,1,0:T(8,128)(2,1)} %get-tuple-element.40.x_ref.attn_ref), custom_call_target="tpu_custom_call" | custom-call | tf_op jit(solution)/shard_map/exchange/pallas_call | solution.py:330
  131.8 39.2 %middle.1 = (bf16[256,768]{1,0:T(8,128)(2,1)}, f32[256,768]{1,0:T(8,128)}, bf16[512,768]{1,0:T(8,128)(2,1)}, f32[8,768]{1,0:T(8,128)}, bf16[4,256,192]{2,1,0:T(8,128)(2,1)}, /*index=5*/bf16[4,768,2560]{2,1,0:T(8,128)(2,1)}) custom-call(bf16[256,768]{1,0:T(8,128)(2,1)} %tok_ref.3, bf16[512,768]{1,0:T(8,128)(2,1)} %bitcast.36, ...), custom_call_target="tpu_custom_call" | custom-call | tf_op jit(solution)/shard_map/middle/pallas_call | solution.py:1003
  171.0 0.7 slice.87
  171.7 16.5 %exchange.3.dattn_ref = bf16[4,256,192]{2,1,0:T(8,128)(2,1)} custom-call(bf16[4,256,192]{2,1,0:T(8,128)(2,1)} %get-tuple-element.47.x_ref), custom_call_target="tpu_custom_call" | custom-call | tf_op jit(solution)/shard_map/exchange/pallas_call | solution.py:330
  188.2 17.1 %self_backward.1 = (bf16[4,256,768]{2,1,0:T(8,128)(2,1)}, bf16[768,704]{1,0:T(8,128)(2,1)}, f32[1,768]{1,0:T(1,128)}, f32[8,128]{1,0:T(8,128)}) custom-call(bf16[4,256,768]{2,1,0:T(8,128)(2,1)} %get-tuple-element.38.tok_ref, bf16[768,704]{1,0:T(8,128)(2,1)} %bitcast.33, f32[1,768]{1,0:T(1,128)} %get-tuple-element.104.g_ref, s32[1024,1]{1,0:T(8,128)} %copy.48.segc_ref, ...), custom_call_target="tpu_custom_call" | custom-call | tf_op jit(solution)/shard_map/self_backward/pallas_call | solution.py:796
  205.3 0.7 convert.8
  206.0 0.2 copy.55
  206.1 0.8 pad.24.clone
  206.9 0.0 copy-start
  206.9 0.0 copy-start.3
  207.0 98.9 %scatter_all.1 = (f32[96,2560]{1,0:T(8,128)}, f32[96,704]{1,0:T(8,128)}, f32[256,768]{1,0:T(8,128)}, f32[128,768]{1,0:T(8,128)}) custom-call(bf16[4,8,96,2560]{3,2,1,0:T(8,128)(2,1)} %bitcast.30, bf16[8,96,704]{2,1,0:T(8,128)(2,1)} %bitcast.34, bf16[4,256,768]{2,1,0:T(8,128)(2,1)} %get-tuple-element.49.u_ref, bf16[4,128,768]{2,1,0:T(8,128)(2,1)} %bitcast.37, ...), custom_call_target="tpu_custom_call" | custom-call | tf_op jit(solution)/shard_map/scatter_all/pallas_call | solution.py:571
  305.9 0.0 copy-start.1
  305.9 1.4 slice_bitcast_fusion.4
  307.3 0.0 copy-done
  307.3 1.4 fusion
  308.7 0.0 copy-start.2
  308.7 0.0 copy-start.5
  308.7 0.0 copy-done.3
  308.7 0.0 copy-done.1
  308.7 1.1 fusion.3
  309.8 0.1 copy-done.2
  309.9 0.1 slice_bitcast_fusion.3
  310.0 0.7 copy.53
  310.6 0.0 copy-done.5
  310.6 0.0 copy-start.4
  310.6 0.9 slice_bitcast_fusion.1
  311.5 0.8 slice_bitcast_fusion
  312.3 0.7 copy.52
  313.1 0.7 copy.51
  313.8 0.0 copy-done.4
  313.8 0.7 copy.58
  (3 shorter events, 0.0 us)
Async XLA Ops:
  0.6 9.9 %copy-start.6 = (s32[1,1024]{1,0:T(1,128)S(1)}, s32[1,1024]{1,0:T(1,128)}, u32[]{:S(2)}) copy-start(s32[1,1024]{1,0:T(1,128)} %segr_ref.3) | copy-start | bytes 12292
  206.9 100.3 %copy-start = (bf16[256,768]{1,0:T(8,128)(2,1)S(1)}, bf16[256,768]{1,0:T(8,128)(2,1)}, u32[]{:S(2)}) copy-start(bf16[256,768]{1,0:T(8,128)(2,1)} %tok_ref.3) | copy-start | bytes 1179652
  206.9 101.7 %copy-start.3 = (f32[256,768]{1,0:T(8,128)S(1)}, f32[256,768]{1,0:T(8,128)}, u32[]{:S(2)}) copy-start(f32[256,768]{1,0:T(8,128)} %get-tuple-element.43) | copy-start | bytes 2359300
  305.9 2.8 copy-start.1
  308.7 1.3 copy-start.2
  308.7 2.0 copy-start.5
  310.6 3.2 %copy-start.4 = (f32[128,768]{1,0:T(8,128)S(1)}, f32[128,768]{1,0:T(8,128)}, u32[]{:S(2)}) copy-start(f32[128,768]{1,0:T(8,128)} %get-tuple-element.128) | copy-start | bytes 1179652

commit v3 on v2

--- a/solution.py
+++ b/solution.py
@@ -15,13 +15,13 @@
 MESH = pl.DeviceIdType.MESH
 VMEM = pl.BlockSpec(memory_space=pltpu.VMEM)
 ANY = pl.BlockSpec(memory_space=pl.ANY)
-LIMIT = 62 * 1024 * 1024
+LIMIT = 63 * 1024 * 1024
 STEP = 256
 SPACE = 2
 PIECE = 32
 TOK0 = 2
 TOKR = 1
-ROWR = 1
+CORE0 = 3
 
 
 def dot(a, b):
@@ -82,17 +82,56 @@
         self.used += 1
         return self.ref.at[self.used - 1]
 
+    def many(self, count):
+        base = self.used
+        self.used += count
+        return lambda n: self.ref.at[base + n]
+
 
 def wait_bytes(ref, sem):
     pltpu.make_async_copy(ref, ref, sem).wait()
 
 
-def enter(nt, nd):
+def row_loop(shape, body):
+    size = 32 if shape[1] <= 256 else 16
+    if shape[0] % size:
+        body(slice(0, shape[0]))
+        return
+
+    def step(n, carry):
+        body(pl.ds(pl.multiple_of(n * size, size), size))
+        return carry
+
+    lax.fori_loop(0, shape[0] // size, step, 0)
+
+
+def add_into(ref, got):
+    if len(ref.shape) == 2:
+
+        def body(at):
+            ref[at, :] = ref[at, :] + got[at, :]
+
+        row_loop(ref.shape, body)
+    else:
+
+        def step(t, carry):
+            ref[t] = ref[t] + got[t]
+            return carry
+
+        lax.fori_loop(0, ref.shape[0], step, 0)
+
+
+def enter(nt, nd, all_tensor=False):
     me_t, me_d = lax.axis_index("tensor"), lax.axis_index("dp")
     bar = pltpu.get_barrier_semaphore()
     bits = nd.bit_length() - 1
     for b in range(bits):
         pl.semaphore_signal(bar, 1, device_id={"dp": flip(me_d, b)}, device_id_type=MESH)
+    if all_tensor:
+        for k in range(1, nt):
+            pl.semaphore_signal(bar, 1, device_id={"tensor": lax.rem(me_t + k, nt)}, device_id_type=MESH)
+        pl.semaphore_wait(bar, bits + nt - 1)
+        return me_t, me_d
 
     @pl.when(me_t > 0)
     def _():
@@ -367,13 +406,7 @@
     def land(k):
         wait_bytes(recv[k], sem[k][1])
         for j, m in enumerate(subsets(order[k + 1 :])):
-            ref = value(flip_all(me, m))
-            got = recv[k].at[j]
-            if len(ref.shape) == 2:
-                ref[...] = (ref[...].astype(F32) + got[...].astype(F32)).astype(BF)
-            else:
-                for t in range(ref.shape[0]):
-                    ref[t] = (ref[t].astype(F32) + got[t].astype(F32)).astype(BF)
+            add_into(value(flip_all(me, m)), recv[k].at[j])
 
     def stage(k):
         def run():
@@ -387,8 +420,11 @@
     return [stage(k) for k in range(count + 1)]
 
 
-def line_scatter(nt, me, value, recv, finish, sends, recvs, after):
-    sem = {(s, b): (sends.take(), recvs.take()) for s in (0, 1) for b in range(nt)}
+def line_scatter(nt, me, value, recv, out, sends, recvs, after):
+    ssem, rsem = sends.many(2 * nt), recvs.many(2 * nt)
+
+    def land(side, b):
+        return recv.at[b + 1 - side]
 
     def hop(z):
         def run():
@@ -401,14 +437,14 @@
                     for b in blocks:
                         ref = value(b)
                         if z > 0:
-                            got = recv.at[side, b]
-                            wait_bytes(got, sem[side, b][1])
-                            ref[...] = (ref[...].astype(F32) + got[...].astype(F32)).astype(BF)
+                            got = land(side, b)
+                            wait_bytes(got, rsem(side * nt + b))
+                            add_into(ref, got)
                         pltpu.make_async_remote_copy(
                             ref,
-                            recv.at[side, b],
-                            sem[side, b][0],
-                            sem[side, b][1],
+                            land(side, b),
+                            ssem(side * nt + b),
+                            rsem(side * nt + b),
                             device_id={"tensor": goal},
                             device_id_type=MESH,
                         ).start()
@@ -416,20 +452,23 @@
         return run
 
     def last():
-        for here in range(nt):
-
-            @pl.when(me == here)
-            def _(here=here):
-                if here > 0:
-                    wait_bytes(recv.at[0, here], sem[0, here][1])
-                if here < nt - 1:
-                    wait_bytes(recv.at[1, here], sem[1, here][1])
-                total = value(here)[...].astype(F32)
-                if here > 0:
-                    total = total + recv.at[0, here][...].astype(F32)
-                if here < nt - 1:
-                    total = total + recv.at[1, here][...].astype(F32)
-                finish(total)
+        own = value(me)
+
+        def first(at):
+            out[at, :] = own[at, :].astype(F32)
+
+        row_loop(out.shape, first)
+        for side, some in ((0, me > 0), (1, me < nt - 1)):
+
+            @pl.when(some)
+            def _(side=side):
+                got = land(side, me)
+                wait_bytes(got, rsem(side * nt + me))
+
+                def more(at):
+                    out[at, :] = out[at, :] + got[at, :].astype(F32)
+
+                row_loop(out.shape, more)
 
     def done():
         for here in range(nt):
@@ -437,23 +476,32 @@
             @pl.when(me == here)
             def _(here=here):
                 for b in range(here + 1, nt):
-                    wait_bytes(recv.at[0, b], sem[0, b][0])
+                    wait_bytes(land(0, b), ssem(b))
                 for b in range(here):
-                    wait_bytes(recv.at[1, b], sem[1, b][0])
+                    wait_bytes(land(1, b), ssem(nt + b))
 
     after.append(done)
     return [hop(z) for z in range(nt - 1)] + [last]
 
 
-def scatter_kernel(
+def backward_kernel(
     nt,
     nd,
+    heads,
+    g_used,
     g_ref,
-    a_ref,
-    u_ref,
     e_ref,
-    gg_ref,
-    tt_ref,
+    gain_in,
+    dmine_ref,
+    tok_ref,
+    wa_ref,
+    g0_ref,
+    segr_ref,
+    bl_ref,
+    tab_ref,
+    qkv_ref,
+    attn_ref,
+    lse_ref,
     g_out,
     a_out,
     u_out,
@@ -464,26 +512,136 @@
     gv, uz, ez, gz = scratch[:4]
     arecv = scratch[4 : 4 + bits]
     grecv = scratch[4 + bits : 4 + 2 * bits]
-    ssem, rsem, lsem = scratch[4 + 2 * bits :]
+    a_ref, u_ref, da_ref, strips, ks, vs, dkt, dvt, dqkv, lines, gain0 = scratch[4 + 2 * bits : 15 + 2 * bits]
+    ssem, rsem, lsem = scratch[15 + 2 * bits :]
     cols = g_ref.shape[3]
     chunks = cols // STEP
     half = STEP // 2
+    block = tok_ref.shape[1]
+    hw = heads * DK
+    width = strips.shape[1]
+    strip, dstrip = strips.at[pl.ds(0, block)], strips.at[pl.ds(block, block)]
+    gat = strips.at[pl.ds(0, 3 * hw), pl.ds(0, tok_ref.shape[2])]
     for c in range(chunks):
         at = pl.ds(c * STEP, STEP)
         pltpu.make_async_copy(g_ref.at[:, :, :, at], gv.at[:, :, :, at], lsem.at[c]).start()
-    me_t, me_d = enter(nt, nd)
+    me_t, me_d = enter(nt, nd, True)
     sends, recvs, after = Sems(ssem), Sems(rsem), []
     orders = [[0] + o[:-1][::-1] for o in bit_orders(bits)]
-    heads = tt_ref.shape[0]
-    wide = a_ref.shape[2]
-    for d in range(nd):
-        a_ref[d, :heads, wide - 128 :] = tt_ref[...].astype(BF)
     jobs = []
+
+    own = pltpu.make_async_copy(dmine_ref.at[me_t], da_ref.at[me_t], lsem.at[chunks])
+    own.start()
+    swaps = []
+    for k in range(1, nt):
+        peer = lax.rem(me_t + k, nt)
+        copy = pltpu.make_async_remote_copy(
+            dmine_ref.at[peer], da_ref.at[me_t], sends.take(), recvs.take(), device_id={"tensor": peer}, device_id_type=MESH
+        )
+        copy.start()
+        swaps.append(copy)
+
+    def swapped():
+        own.wait()
+        for copy in swaps:
+            copy.wait_recv()
+
+    after.extend(copy.wait_send for copy in swaps)
+
+    line, hot = bias_lines(bl_ref, tab_ref)
+
+    def rows_of(i):
+        return slice(i * block, (i + 1) * block)
+
+    def head_start(h):
+        build_strip(strip, line[h : h + 1, :])
+        dstrip[...] = jnp.zeros_like(dstrip)
+        dkt[...] = jnp.zeros_like(dkt)
+        dvt[...] = jnp.zeros_like(dvt)
+        for i in range(nt):
+            ks[rows_of(i), :] = qkv_ref[i, :, hw + h * DK : hw + (h + 1) * DK]
+            vs[rows_of(i), :] = qkv_ref[i, :, 2 * hw + h * DK : 2 * hw + (h + 1) * DK]
+
+    def piece(h, i):
+        mine = rows_of(i)
+        seen = (i + 1) * block
+        off = (nt - 1 - i) * block
+        part = slice(h * DK, (h + 1) * DK)
+        q = qkv_ref[i, :, part]
+        da = da_ref[i, :, part]
+        delta = jnp.sum(da.astype(F32) * attn_ref[i, :, part].astype(F32), axis=1, keepdims=True)
+        s = dot_nt(q, ks[:seen, :])
+        s = s + strip[:, off : off + seen]
+        s = jnp.where(column(segr_ref[:, mine]) == segr_ref[:, :seen], s, MASKED)
+        p = jnp.exp(s - lse_ref[mine, h : h + 1])
+        dp = dot_nt(da, vs[:seen, :])
+        ds = p * (dp - delta)
+        low = ds.astype(BF)
+        dqkv[mine, part] = dot(low, ks[:seen, :]).astype(BF)
+        dkt[:, :seen] += dot_tn(q, low)
+        dvt[:, :seen] += dot_tn(da, p.astype(BF))
+        dstrip[:, off : off + seen] += ds
+
+    def head_end(h):
+        for i in range(nt):
+            dqkv[rows_of(i), hw + h * DK : hw + (h + 1) * DK] = dkt[:, rows_of(i)].T.astype(BF)
+            dqkv[rows_of(i), 2 * hw + h * DK : 2 * hw + (h + 1) * DK] = dvt[:, rows_of(i)].T.astype(BF)
+        n = block // 2
+        while n >= 8:
+            dstrip[0:n, :] = dstrip[0:n, :] + pltpu.roll(dstrip[n : 2 * n, :], width - n, 1)
+            n //= 2
+        x = dstrip[0:8, :]
+        row = lax.broadcasted_iota(jnp.int32, x.shape, 0)
+        for b in range(3):
+            x = jnp.where((row >> b) % 2 == 1, pltpu.roll(x, width - (1 << b), 1), x)
+        lines[h : h + 1, :] = jnp.sum(x, axis=0, keepdims=True)
+
+    def rows_end(i):
+        mine = rows_of(i)
+        x = tok_ref[i].astype(F32)
+        hat = x * norm_scale(x)
+        more = dot_tn(dqkv[mine, :], (hat * g0_ref[...]).astype(BF))
+        gat[...] = more if i == 0 else gat[...] + more
+        u = dot_nt(dqkv[mine, :], wa_ref[:, : 3 * hw])
+        gain0[...] += jnp.sum(u * hat, axis=0, keepdims=True)
+        u_ref[i] = u.astype(BF)
+
+    def finish():
+        table = lax.dot_general(
+            lines[...],
+            hot.astype(F32),
+            (((1,), (1,)), ((), ())),
+            precision=lax.Precision.HIGHEST,
+            preferred_element_type=F32,
+        )
+        table = jnp.concatenate([table, jnp.zeros((8, 128 - table.shape[1]), F32)], axis=1).astype(BF)
+        ga = gat[...].T.astype(BF)
+        part = ga.shape[0] // nd
+        for d in range(nd):
+            a_ref[d, :, : 3 * hw] = ga[d * part : (d + 1) * part]
+            a_ref[d, :, 3 * hw :] = jnp.zeros((part, 128), BF)
+            a_ref[d, :8, 3 * hw :] = table
+
+    def add_gains():
+        at = g_used - (cols - 128)
+        row = lax.broadcasted_iota(jnp.int32, (128, gain0.shape[1]), 0)
+        gains = jnp.where(row == at, gain0[...], 0.0)
+        gains = gains + jnp.where(row == at + 1, gain_in[0:1, :], 0.0) + jnp.where(row == at + 2, gain_in[1:2, :], 0.0)
+        gains = gains.T.astype(BF)
+        part = gains.shape[0] // nd
+
+        def step(t, carry):
+            for d in range(nd):
+                gv[t, d, :, cols - 128 :] = gv[t, d, :, cols - 128 :] + gains[d * part : (d + 1) * part]
+            return carry
+
+        lax.fori_loop(0, nt, step, 0)
+
+    lines[...] = jnp.zeros_like(lines)
+    gain0[...] = jnp.zeros_like(gain0)
 
     def a_done():
         a_out[...] = a_ref[me_d].astype(F32)
-
-    a_job = cube_scatter(nd, me_d, orders[0], lambda d: a_ref.at[d], arecv, sends, recvs, after) + [a_done]
 
     def chunk_job(c):
         first = c * STEP
@@ -502,16 +660,12 @@
                     after,
                 )
             )
-
-        def finish(total):
-            g_out[:, first : first + STEP] = total
-
         z = line_scatter(
             nt,
             me_t,
             lambda b: gv.at[b, me_d, :, pl.ds(first, STEP)],
             gz.at[c],
-            finish,
+            g_out.at[:, pl.ds(first, STEP)],
             sends,
             recvs,
             after,
@@ -521,9 +675,7 @@
             at = pl.ds(first, STEP)
             pltpu.make_async_copy(g_ref.at[:, :, :, at], gv.at[:, :, :, at], lsem.at[c]).wait()
             if c == chunks - 1:
-                for t in range(nt):
-                    for d in range(nd):
-                        gv[t, d, :, cols - 128 :] = gv[t, d, :, cols - 128 :] + gg_ref[d]
+                add_gains()
             for q in cubes:
                 q[0]()
 
@@ -543,72 +695,95 @@
 
     def row_job(ref, recv, out, n):
         at = pl.ds(n * PIECE, PIECE)
-
-        def finish(total):
-            out[at, :] = total
-
-        return line_scatter(nt, me_t, lambda b: ref.at[b, at], recv.at[:, :, at], finish, sends, recvs, after)
+        return line_scatter(nt, me_t, lambda b: ref.at[b, at], recv.at[:, at], out.at[at], sends, recvs, after)
 
     ticks = [SPACE * k for k in range(bits)] + [SPACE * bits + k for k in range(nt)]
-    jobs.append((0, a_job, [SPACE * k for k in range(bits + 1)] + [SPACE * bits]))
     for c in range(chunks):
-        jobs.append((c, chunk_job(c), ticks))
-    number = 0
-    for ref, recv, out in ((u_ref, uz, u_out), (e_ref, ez, e_out)):
-        for n in range(out.shape[0] // PIECE):
-            jobs.append((number // ROWR, row_job(ref, recv, out, n), list(range(nt))))
-            number += 1
+        jobs.append((min(c, chunks - 1), chunk_job(c), ticks))
+    for n in range(e_out.shape[0] // PIECE):
+        jobs.append((n, row_job(e_ref, ez, e_out, n), list(range(nt))))
+    compute = [(CORE0 - 1, partial(head_start, 0)), (CORE0, swapped)]
+    for h in range(heads):
+        if h > 0:
+            compute.append((CORE0 + h, partial(head_start, h)))
+        compute += [(CORE0 + h, partial(piece, h, i)) for i in range(nt)]
+        compute.append((CORE0 + h, partial(head_end, h)))
+    ready = CORE0 + heads
+    compute += [(ready, partial(rows_end, i)) for i in range(nt)]
+    compute.append((ready, finish))
+    for tick, fn in compute:
+        jobs.append((tick, [fn], [0]))
+    a_job = cube_scatter(nd, me_d, orders[0], lambda d: a_ref.at[d], arecv, sends, recvs, after) + [a_done]
+    jobs.append((ready + 1, a_job, [SPACE * k for k in range(bits + 1)] + [SPACE * bits]))
+    for n in range(u_out.shape[0] // PIECE):
+        jobs.append((ready + 1 + n, row_job(u_ref, uz, u_out, n), list(range(nt))))
     run_jobs(jobs, after)
 
 
-def scatter_all(nt, nd, g, a, u, e, gg, tt):
+def backward_all(nt, nd, heads, used, g, e, gain12, dmine, tok, wa, g0, segr, bl, tab, qkv, attn, lse):
     bits = nd.bit_length() - 1
     rows, cols = g.shape[2:]
-    wide = a.shape[2]
+    block, width = tok.shape[1:]
+    length = nt * block
+    wide = wa.shape[1]
+    hw = heads * DK
     chunks = cols // STEP
-    lines = chunks + (u.shape[1] + e.shape[1]) // PIECE
-    total = lines * 2 * nt + (2 * chunks + 1) * bits
+    lines = chunks + (block + e.shape[1]) // PIECE
+    total = lines * 2 * nt + (2 * chunks + 1) * bits + nt - 1
     return pl.pallas_call(
-        partial(scatter_kernel, nt, nd),
+        partial(backward_kernel, nt, nd, heads, used),
         out_shape=(
             jax.ShapeDtypeStruct((rows, cols), F32),
             jax.ShapeDtypeStruct((rows, wide), F32),
-            jax.ShapeDtypeStruct(u.shape[1:], F32),
+            jax.ShapeDtypeStruct((block, width), F32),
             jax.ShapeDtypeStruct(e.shape[1:], F32),
         ),
-        in_specs=[ANY] + [VMEM] * 5,
+        in_specs=[ANY] + [VMEM] * 12,
         out_specs=(VMEM,) * 4,
         scratch_shapes=[
             pltpu.VMEM((nt, nd, rows, cols), BF),
-            pltpu.VMEM((2,) + u.shape, BF),
-            pltpu.VMEM((2,) + e.shape, BF),
-            pltpu.VMEM((chunks, 2, nt, rows, STEP), BF),
+            pltpu.VMEM((nt + 1, block, width), BF),
+            pltpu.VMEM((nt + 1,) + e.shape[1:], BF),
+            pltpu.VMEM((chunks, nt + 1, rows, STEP), BF),
         ]
         + [pltpu.VMEM((1 << (bits - 1 - k), rows, wide), BF) for k in range(bits)]
         + [pltpu.VMEM((2 * chunks, 1 << (bits - 1 - k), nt, rows, STEP // 2), BF) for k in range(bits)]
         + [
+            pltpu.VMEM((nd, rows, wide), BF),
+            pltpu.VMEM((nt, block, width), BF),
+            pltpu.VMEM((nt, block, hw), BF),
+            pltpu.VMEM((max(2 * block, 3 * hw), length + block), F32),
+            pltpu.VMEM((length, DK), BF),
+            pltpu.VMEM((length, DK), BF),
+            pltpu.VMEM((DK, length), F32),
+            pltpu.VMEM((DK, length), F32),
+            pltpu.VMEM((length, 3 * hw), BF),
+            pltpu.VMEM((8, length + block), F32),
+            pltpu.VMEM((1, width), F32),
             pltpu.SemaphoreType.DMA((total,)),
             pltpu.SemaphoreType.DMA((total,)),
-            pltpu.SemaphoreType.DMA((chunks,)),
+            pltpu.SemaphoreType.DMA((chunks + 1,)),
         ],
         compiler_params=pltpu.CompilerParams(collective_id=1, has_side_effects=True, vmem_limit_bytes=LIMIT),
-        name="scatter_all",
-    )(g, a, u, e, gg, tt)
-
-
-def build_strips(strip, line, heads):
-    block = strip.shape[1]
-    width = strip.shape[2]
+        name="backward_all",
+    )(g, e, gain12, dmine, tok, wa, g0, segr, bl, tab, qkv, attn, lse)
+
+
+def column(row):
+    return jnp.broadcast_to(row, (8, row.shape[1])).T[:, 0:1]
+
+
+def build_strip(strip, x):
+    block, width = strip.shape
     row = lax.broadcasted_iota(jnp.int32, (8, width), 0)
-    for h in range(heads):
-        x = jnp.broadcast_to(line[h : h + 1, :], (8, width))
-        for b in range(3):
-            x = jnp.where((row >> b) % 2 == 1, pltpu.roll(x, 1 << b, 1), x)
-        strip[h, 0:8, :] = x
-        n = 8
-        while n < block:
-            strip[h, n : 2 * n, :] = pltpu.roll(strip[h, 0:n, :], n, 1)
-            n *= 2
+    x = jnp.broadcast_to(x, (8, width))
+    for b in range(3):
+        x = jnp.where((row >> b) % 2 == 1, pltpu.roll(x, 1 << b, 1), x)
+    strip[0:8, :] = x
+    n = 8
+    while n < block:
+        strip[n : 2 * n, :] = pltpu.roll(strip[0:n, :], n, 1)
+        n *= 2
 
 
 def bias_lines(bl_ref, tab_ref):
@@ -620,12 +795,13 @@
 
 
 def self_forward_kernel(
-    heads, tok_ref, wa_ref, g_ref, segc_ref, segr_ref, bl_ref, tab_ref, qkv_ref, attn_ref, lse_ref, strip, qs, ks, vs, os
+    heads, tok_ref, wa_ref, g_ref, segr_ref, bl_ref, tab_ref, qkv_ref, attn_ref, lse_ref, strip, qs, ks, vs, os, lses
 ):
     nt, block = tok_ref.shape[:2]
     hw = heads * DK
     line, _ = bias_lines(bl_ref, tab_ref)
-    build_strips(strip, line, heads)
+    for h in range(heads):
+        build_strip(strip.at[h], line[h : h + 1, :])
     for i in range(nt):
         x = tok_ref[i].astype(F32)
         n = (x * norm_scale(x) * g_ref[...]).astype(BF)
@@ -642,22 +818,24 @@
             seen = (i + 1) * block
             s = dot_nt(qs[h, mine, :], ks[h, :seen, :])
             s = s + strip[h, :, (nt - 1 - i) * block : (nt - 1 - i) * block + seen]
-            s = jnp.where(segc_ref[mine, :] == segr_ref[:, :seen], s, MASKED)
+            s = jnp.where(column(segr_ref[:, mine]) == segr_ref[:, :seen], s, MASKED)
             top = jnp.max(s, axis=-1, keepdims=True)
             p = jnp.exp(s - top)
             total = jnp.sum(p, axis=-1, keepdims=True)
             o = dot(p.astype(BF), vs[h, :seen, :]) / total
             os[h, mine, :] = o
-            lse_ref[h, mine, :] = top + jnp.log(total)
+            lses[h, mine, :] = top + jnp.log(total)
         return carry
 
     lax.fori_loop(0, heads, head, 0)
     for i in range(nt):
         mine = slice(i * block, (i + 1) * block)
         attn_ref[i] = jnp.concatenate([os[h, mine, :] for h in range(heads)], axis=1).astype(BF)
-
-
-def self_forward(heads, tok, wa, g, segc, segr, bl, tab):
+        for h in range(heads):
+            lse_ref[mine, h : h + 1] = lses[h, mine, :]
+
+
+def self_forward(heads, tok, wa, g, segr, bl, tab):
     nt, block, width = tok.shape
     length = nt * block
     hw = heads * DK
@@ -666,151 +844,16 @@
         out_shape=(
             jax.ShapeDtypeStruct((nt, block, 3 * hw), BF),
             jax.ShapeDtypeStruct((nt, block, hw), BF),
-            jax.ShapeDtypeStruct((heads, length, 1), F32),
+            jax.ShapeDtypeStruct((length, 8), F32),
         ),
-        in_specs=[VMEM] * 7,
+        in_specs=[VMEM] * 6,
         out_specs=(VMEM,) * 3,
         scratch_shapes=[pltpu.VMEM((heads, block, length + block), F32)]
         + [pltpu.VMEM((heads, length, DK), BF)] * 3
-        + [pltpu.VMEM((heads, length, DK), F32)],
+        + [pltpu.VMEM((heads, length, DK), F32), pltpu.VMEM((heads, length, 1), F32)],
         compiler_params=pltpu.CompilerParams(vmem_limit_bytes=LIMIT),
         name="self_forward",
-    )(tok, wa, g, segc, segr, bl, tab)
-
-
-def self_backward_kernel(
-    heads,
-    tok_ref,
-    wa_ref,
-    g_ref,
-    segc_ref,
-    segr_ref,
-    bl_ref,
-    tab_ref,
-    qkv_ref,
-    attn_ref,
-    lse_ref,
-    dattn_ref,
-    u_ref,
-    ga_ref,
-    gain_ref,
-    table_ref,
-    strip,
-    dstrip,
-    qs,
-    ks,
-    vs,
-    das,
-    delta,
-    dq,
-    dkt,
-    dvt,
-    norms,
-    dqkv,
-):
-    nt, block = tok_ref.shape[:2]
-    hw = heads * DK
-    length = nt * block
-    line, hot = bias_lines(bl_ref, tab_ref)
-    build_strips(strip, line, heads)
-    for i in range(nt):
-        mine = slice(i * block, (i + 1) * block)
-        y = qkv_ref[i]
-        da = dattn_ref[i]
-        prod = da.astype(F32) * attn_ref[i].astype(F32)
-        for h in range(heads):
-            part = slice(h * DK, (h + 1) * DK)
-            for which, ref in enumerate((qs, ks, vs)):
-                at = which * hw + h * DK
-                ref[h, mine, :] = y[:, at : at + DK]
-            das[h, mine, :] = da[:, part]
-            delta[h, mine, :] = jnp.sum(prod[:, part], axis=1, keepdims=True)
-    dstrip[...] = jnp.zeros_like(dstrip)
-    dkt[...] = jnp.zeros_like(dkt)
-    dvt[...] = jnp.zeros_like(dvt)
-
-    def head(h, carry):
-        for i in range(nt):
-            mine = slice(i * block, (i + 1) * block)
-            seen = (i + 1) * block
-            off = (nt - 1 - i) * block
-            q = qs[h, mine, :]
-            da = das[h, mine, :]
-            s = dot_nt(q, ks[h, :seen, :])
-            s = s + strip[h, :, off : off + seen]
-            s = jnp.where(segc_ref[mine, :] == segr_ref[:, :seen], s, MASKED)
-            p = jnp.exp(s - lse_ref[h, mine, :])
-            dp = dot_nt(da, vs[h, :seen, :])
-            ds = p * (dp - delta[h, mine, :])
-            low = ds.astype(BF)
-            dq[h, mine, :] = dot(low, ks[h, :seen, :])
-            dkt[h, :, :seen] += dot_tn(q, low)
-            dvt[h, :, :seen] += dot_tn(da, p.astype(BF))
-            dstrip[h, :, off : off + seen] += ds
-        return carry
-
-    lax.fori_loop(0, heads, head, 0)
-    lines = []
-    for h in range(heads):
-        n = block // 2
-        while n >= 8:
-            dstrip[h, 0:n, :] = dstrip[h, 0:n, :] + pltpu.roll(dstrip[h, n : 2 * n, :], length + block - n, 1)
-            n //= 2
-        x = dstrip[h, 0:8, :]
-        row = lax.broadcasted_iota(jnp.int32, x.shape, 0)
-        for b in range(3):
-            x = jnp.where((row >> b) % 2 == 1, pltpu.roll(x, length + block - (1 << b), 1), x)
-        lines.append(jnp.sum(x, axis=0, keepdims=True))
-    lines = jnp.concatenate(lines + [jnp.zeros((8 - heads, length + block), F32)], axis=0)
-    table = lax.dot_general(
-        lines,
-        hot.astype(F32),
-        (((1,), (1,)), ((), ())),
-        precision=lax.Precision.HIGHEST,
-        preferred_element_type=F32,
-    )
-    table_ref[...] = jnp.concatenate([table, jnp.zeros((8, 128 - table.shape[1]), F32)], axis=1)
-    gain = jnp.zeros(gain_ref.shape, F32)
-    for i in range(nt):
-        mine = slice(i * block, (i + 1) * block)
-        pieces = [dq[h, mine, :] for h in range(heads)]
-        pieces += [dkt[h, :, mine].T for h in range(heads)]
-        pieces += [dvt[h, :, mine].T for h in range(heads)]
-        low = jnp.concatenate(pieces, axis=1).astype(BF)
-        dqkv[mine, :] = low
-        x = tok_ref[i].astype(F32)
-        hat = x * norm_scale(x)
-        norms[mine, :] = (hat * g_ref[...]).astype(BF)
-        u = dot_nt(low, wa_ref[:, : 3 * hw])
-        gain = gain + jnp.sum(u * hat, axis=0, keepdims=True)
-        u_ref[i] = u.astype(BF)
-    gain_ref[...] = gain
-    ga_ref[:, : 3 * hw] = dot_tn(norms[...], dqkv[...]).astype(BF)
-    ga_ref[:, 3 * hw :] = jnp.zeros((ga_ref.shape[0], ga_ref.shape[1] - 3 * hw), BF)
-
-
-def self_backward(heads, tok, wa, g, segc, segr, bl, tab, qkv, attn, lse, dattn):
-    nt, block, width = tok.shape
-    length = nt * block
-    hw = heads * DK
-    return pl.pallas_call(
-        partial(self_backward_kernel, heads),
-        out_shape=(
-            jax.ShapeDtypeStruct((nt, block, width), BF),
-            jax.ShapeDtypeStruct(wa.shape, BF),
-            jax.ShapeDtypeStruct((1, width), F32),
-            jax.ShapeDtypeStruct((8, 128), F32),
-        ),
-        in_specs=[VMEM] * 11,
-        out_specs=(VMEM,) * 4,
-        scratch_shapes=[pltpu.VMEM((heads, block, length + block), F32)] * 2
-        + [pltpu.VMEM((heads, length, DK), BF)] * 4
-        + [pltpu.VMEM((heads, length, 1), F32), pltpu.VMEM((heads, length, DK), F32)]
-        + [pltpu.VMEM((heads, DK, length), F32)] * 2
-        + [pltpu.VMEM((length, width), BF), pltpu.VMEM((length, 3 * hw), BF)],
-        compiler_params=pltpu.CompilerParams(vmem_limit_bytes=LIMIT),
-        name="self_backward",
-    )(tok, wa, g, segc, segr, bl, tab, qkv, attn, lse, dattn)
+    )(tok, wa, g, segr, bl, tab)
 
 
 def middle_kernel(
@@ -1080,29 +1123,30 @@
     )[None, :]
     tab = jnp.pad(bias_table.T, ((0, 8 - heads), (0, 0)))
     segr = segments
-    segc = segments.T
     g0 = gains[0:1]
-    qkv, attn, lse = self_forward(heads, tok_all, wa_full, g0, segc, segr, bl, tab)
+    qkv, attn, lse = self_forward(heads, tok_all, wa_full, g0, segr, bl, tab)
     mine = exchange(nt, attn, 2)
     layer_out, grad_one, denc, gain12, dmine, gb = middle(
         heads, ff, tokens, enc_all.reshape(nt * encoder.shape[0], width), mine, out_grad, gains, wb_full
     )
-    dattn = exchange(nt, dmine, 3)
-    u, ga, gain0, table = self_backward(
-        heads, tok_all, wa_full, g0, segc, segr, bl, tab, qkv, attn, lse, dattn
-    )
-    gg = jnp.concatenate([gain0, gain12[0:2]], axis=0).T.astype(BF)
-    lane = used - (cols - 128)
-    gg = jnp.pad(gg, ((0, 0), (lane, 128 - lane - 3))).reshape(nd, part, 128)
-    gsum, asum, usum, esum = scatter_all(
+    gsum, asum, usum, esum = backward_all(
         nt,
         nd,
+        heads,
+        used,
         gb.reshape(nt, nd, part, cols),
-        ga.reshape(nd, part, wa.shape[1]),
-        u,
         denc.reshape((nt,) + encoder.shape),
-        gg,
-        table,
+        gain12,
+        dmine,
+        tok_all,
+        wa_full,
+        g0,
+        segr,
+        bl,
+        tab,
+        qkv,
+        attn,
+        lse,
     )
     x = tokens.astype(F32)
     back, _ = norm_back(x, norm_scale(x), g0, usum)

time: 321 us -> 301 us (0.938)
  Pallas kernels: 289 us -> 272 us
    pallas_call x2 -> x1, Pallas kernels: 31.5 us -> 15 us  [exchange(): pl.pallas_call(partial(exchange_kernel, nt), out_shape=jax.ShapeDtypeStru...]
    pallas_call x2 -> x1, Pallas kernels: 116 us -> 115 us  [backward_all(): pl.pallas_call(partial(backward_kernel, nt, nd, heads, used), out_shape=(...]
    unnamed x27 -> x22, local copies, waits for them, and re-layouts: 6.93 us -> 6.63 us
where the time goes in v3:
time: 301 us; the launch traced here: 295 us
  Pallas kernels  272 us (90%)
  local copies, waits for them, and re-layouts  15.7 us (5%)
  other arithmetic  6.34 us (2%)
    pallas_call x1, Pallas kernels, backward_all(): pl.pallas_call(partial(backward_kernel, nt, nd, heads, used), out_shape=(...  115 us
    pallas_call x1, Pallas kernels, gather_all(): pl.pallas_call(partial(gather_kernel, nt, nd), out_shape=(jax.ShapeDtypeS...  91.1 us
    pallas_call x1, Pallas kernels, middle(): pl.pallas_call(partial(middle_kernel, heads, ff), out_shape=(jax.ShapeDty...  39.2 us
    pallas_call x1, Pallas kernels, exchange(): pl.pallas_call(partial(exchange_kernel, nt), out_shape=jax.ShapeDtypeStru...  15 us
    pallas_call x1, Pallas kernels, self_forward(): pl.pallas_call(partial(self_forward_kernel, heads), out_shape=(jax.ShapeD...  11.7 us
    unnamed x22, local copies, waits for them, and re-layouts  6.63 us

profile of v3, /device:TPU:0, one launch (start us, length us, event | category | flops | bytes accessed | tf_op | source)
XLA Modules:
  0.0 294.9 jit_solution(13725326701063009979)
XLA Ops:
  0.6 0.8 slice.55
  1.4 0.1 reverse.1
  1.5 0.1 slice.79
  1.6 1.3 pad.18.tab_ref
  2.8 0.8 reverse
  3.6 0.1 slice.78
  3.7 0.1 concatenate.11
  3.8 0.6 broadcast_in_dim.9.bl_ref
  4.4 0.8 copy.43
  5.2 0.9 copy.45
  6.1 0.9 copy.44
  7.0 1.6 fusion.5.wa_ref
  8.6 1.1 concatenate.10
  9.7 0.8 pad.17.wb_ref
  10.5 91.1 %gather_all.1 = (bf16[4,256,768]{2,1,0:T(8,128)(2,1)}, bf16[4,128,768]{2,1,0:T(8,128)(2,1)}, bf16[8,96,704]{2,1,0:T(8,128)(2,1)}, bf16[4,8,96,2560]{3,2,1,0:T(8,128)(2,1)}) custom-call(bf16[256,768]{1,0:T(8,128)(2,1)} %tok_ref.3, bf16[128,768]{1,0:T(8,128)(2,1)} %enc_ref.1, bf16[96,704]{1,0:T(8,128)(2,1)} %fusion.5.wa_ref, bf16[96,2560]{1,0:T(8,128)(2,1)} %pad.17.wb_ref), custom_call_target="tpu_custom_call" | custom-call | tf_op jit(solution)/shard_map/gather_all/pallas_call | solution.py:327
  101.6 1.0 slice_convert_fusion
  102.7 0.1 copy.51
  102.8 0.6 slice_reduce_fusion
  103.4 0.6 pad.19.gains_ref
  104.0 11.7 %self_forward.1 = (bf16[4,256,576]{2,1,0:T(8,128)(2,1)}, bf16[4,256,192]{2,1,0:T(8,128)(2,1)}, f32[1024,8]{1,0:T(8,128)}) custom-call(bf16[4,256,768]{2,1,0:T(8,128)(2,1)} %get-tuple-element.34.tok_ref, bf16[768,704]{1,0:T(8,128)(2,1)} %bitcast.27, f32[1,768]{1,0:T(1,128)} %get-tuple-element.96.g_ref.g0_ref, s32[1,1024]{1,0:T(1,128)} %segr_ref.3, ...), custom_call_target="tpu_custom_call" | custom-call | tf_op jit(solution)/shard_map/self_forward/pallas_call | solution.py:842
  115.8 15.0 %exchange.1.attn_ref = bf16[4,256,192]{2,1,0:T(8,128)(2,1)} custom-call(bf16[4,256,192]{2,1,0:T(8,128)(2,1)} %get-tuple-element.36.x_ref.attn_ref), custom_call_target="tpu_custom_call" | custom-call | tf_op jit(solution)/shard_map/exchange/pallas_call | solution.py:369
  130.7 39.2 %middle.1 = (bf16[256,768]{1,0:T(8,128)(2,1)}, f32[256,768]{1,0:T(8,128)}, bf16[512,768]{1,0:T(8,128)(2,1)}, f32[8,768]{1,0:T(8,128)}, bf16[4,256,192]{2,1,0:T(8,128)(2,1)}, /*index=5*/bf16[4,768,2560]{2,1,0:T(8,128)(2,1)}) custom-call(bf16[256,768]{1,0:T(8,128)(2,1)} %tok_ref.3, bf16[512,768]{1,0:T(8,128)(2,1)} %bitcast.29, ...), custom_call_target="tpu_custom_call" | custom-call | tf_op jit(solution)/shard_map/middle/pallas_call | solution.py:1046
  170.0 0.0 copy-start
  170.0 114.7 %backward_all.1 = (f32[96,2560]{1,0:T(8,128)}, f32[96,704]{1,0:T(8,128)}, f32[256,768]{1,0:T(8,128)}, f32[128,768]{1,0:T(8,128)}) custom-call(bf16[4,8,96,2560]{3,2,1,0:T(8,128)(2,1)} %bitcast.25, bf16[4,128,768]{2,1,0:T(8,128)(2,1)} %bitcast.30, f32[8,768]{1,0:T(8,128)} %get-tuple-element.42.gain_in, bf16[4,256,192]{2,1,0:T(8,128)(2,1)} %get-tuple-element.43.dmine_ref, ...), custom_call_target="tpu_custom_call" | custom-call | tf_op jit(solution)/shard_map/backward_all/pallas_call | solution.py:733
  284.7 0.0 copy-start.1
  284.7 1.4 slice_bitcast_fusion.4
  286.1 0.0 copy-done
  286.1 1.4 fusion
  287.4 0.0 copy-start.2
  287.5 0.0 copy-start.4
  287.5 0.0 copy-done.1
  287.5 2.3 fusion.3
  289.8 0.0 copy-done.2
  289.8 0.1 slice_bitcast_fusion.3
  289.9 0.7 copy.49
  290.5 0.0 copy-done.4
  290.5 0.0 copy-start.3
  290.5 0.9 slice_bitcast_fusion.1
  291.4 0.8 slice_bitcast_fusion
  292.2 0.7 copy.48
  293.0 0.7 copy.47
  293.7 0.0 copy-done.3
  293.7 0.7 copy.53
  (2 shorter events, 0.0 us)
Async XLA Ops:
  170.0 116.1 %copy-start = (bf16[256,768]{1,0:T(8,128)(2,1)S(1)}, bf16[256,768]{1,0:T(8,128)(2,1)}, u32[]{:S(2)}) copy-start(bf16[256,768]{1,0:T(8,128)(2,1)} %tok_ref.3) | copy-start | bytes 1179652
  284.7 2.8 copy-start.1
  287.4 2.4 copy-start.2
  287.5 3.1 %copy-start.4 = (f32[96,704]{1,0:T(8,128)S(1)}, f32[96,704]{1,0:T(8,128)}, u32[]{:S(2)}) copy-start(f32[96,704]{1,0:T(8,128)} %get-tuple-element.48) | copy-start | bytes 811012
  290.5 3.2 %copy-start.3 = (f32[128,768]{1,0:T(8,128)S(1)}, f32[128,768]{1,0:T(8,128)}, u32[]{:S(2)}) copy-start(f32[128,768]{1,0:T(8,128)} %get-tuple-element.120) | copy-start | bytes 1179652
